TPU v7x, 32 devices: a whole 2x2x4 slice. The times are simulated.
32 devices in a mesh: pipe: 4 (over x, core), fsdp: 8 (over z, y).
Axes of the slice: x: 2, y: 2, z: 4, core: 2. Of those that a mesh axis runs over, the one named last changes fastest.
Arguments:
- saved: bfloat16 [4, 8, 3, 64, 4096], P('pipe', 'fsdp'), may hold values from -6 to 6
- cot_in: bfloat16 [4, 8, 64, 4096], P('pipe', 'fsdp'), may hold values from -6 to 6
- weights: bfloat16 [2, 4, 4096, 1024], P(None, 'pipe', 'fsdp'), may hold values from -0.09375 to 0.09375
- gains: bfloat16 [2, 4, 4096], P(None, 'pipe', 'fsdp'), may hold values from 0.099609375 to 1.8984375
- lengths: int32 [4, 8], P(None, 'fsdp'), may hold values from 1 to 64, 384 in all within a row
- segments: int32 [4, 8, 64], P(None, 'fsdp'), may hold values from 0 to 3, never falling along the last dimension, each value on 1 to 32 neighbouring positions
Outputs:
- cot_out: bfloat16 [4, 8, 64, 4096], P('pipe', 'fsdp')
- grad_kv: bfloat16 [2, 4, 4096, 1024], P(None, 'pipe', 'fsdp')
- grad_gain: bfloat16 [2, 4, 4096], P(None, 'pipe', 'fsdp')
Inputs may be any that keep to these rules, and one draw needn't show every extreme that they name: The lengths of the 8 micro-batches of one j sum to 384 and the largest is 64. `segments`: document numbers never fall along the slots; a document spans at most 32 slots.
All inputs are finite; a program needn't handle non-finite values. No bound on the sum of `lengths` on one device may be relied on, other than what follows from the above.
Results may differ from a plain program's by a relative error of at most 0.02.
Values may be sent and summed in bfloat16 or wider, within the bound.
A program may use at most 128 MiB of HBM per device.

v0:
```python
import jax
import jax.numpy as jnp
from jax import lax
from jax.sharding import PartitionSpec as P

D = 4096
HEAD_SIZE = 128
KEY_VALUE_HEADS = 4
TICKS = 3


EPS = 1e-05


def passed_along(value, axis, by):
    size = lax.axis_size(axis)
    return lax.ppermute(value, axis, [(i, (i + by) % size) for i in range(size)])


def normalize(resid, gain):
    factor = lax.rsqrt(jnp.mean(resid * resid, axis=-1, keepdims=True) + EPS)
    return resid * factor * gain


def attend(resid, normalized_input, key_value_pair, length, segment):
    item_count = resid.shape[0]
    model_width = resid.shape[1]
    query_groups = model_width // HEAD_SIZE // KEY_VALUE_HEADS
    query_rows = normalized_input.astype(jnp.bfloat16).reshape(
        item_count, KEY_VALUE_HEADS, query_groups, HEAD_SIZE
    )
    key_rows = (
        key_value_pair[:, : KEY_VALUE_HEADS * HEAD_SIZE]
        .astype(jnp.bfloat16)
        .reshape(item_count, KEY_VALUE_HEADS, HEAD_SIZE)
    )
    value_rows = (
        key_value_pair[:, KEY_VALUE_HEADS * HEAD_SIZE :]
        .astype(jnp.bfloat16)
        .reshape(item_count, KEY_VALUE_HEADS, HEAD_SIZE)
    )
    scores = jnp.einsum(
        "pkgd,qkd->kgpq", query_rows, key_rows, preferred_element_type=jnp.float32
    ) * HEAD_SIZE ** (-0.5)
    place = jnp.arange(item_count, dtype=jnp.int32)
    allowed = (
        (segment[:, None] == segment[None, :])
        & (place[None, :] <= place[:, None])
        & (place[None, :] < length)
    )
    allowed = allowed | (place[:, None] == place[None, :])
    scores = jnp.where(allowed, scores, -1e30)
    peak = jnp.max(scores, axis=-1, keepdims=True)
    expo = jnp.exp(scores - peak)
    probs = (expo / jnp.sum(expo, axis=-1, keepdims=True)).astype(jnp.bfloat16)
    mixed = jnp.einsum(
        "kgpq,qkd->pkgd", probs, value_rows, preferred_element_type=jnp.float32
    ).reshape(item_count, model_width)
    valid = (place < length).astype(jnp.float32)
    return resid + mixed * valid[:, None]


def attend_back(resid, normalized_input, key_value_pair, cotangent, length, segment):

    def inner(first, second, third):
        return attend(first, second, third, length, segment)

    _, pull = jax.vjp(inner, resid, normalized_input, key_value_pair)
    direct, normed_cot, keyval_cot = pull(cotangent.astype(jnp.float32))
    return (direct, normed_cot, keyval_cot.astype(jnp.bfloat16))


def times_transposed(left, right):
    return lax.dot_general(
        left, right, (((1,), (1,)), ((), ())), preferred_element_type=jnp.float32
    )


def body(saved, cot_in, weights, gains, lengths, segments):
    sections = lax.axis_size("pipe")
    section = lax.axis_index("pipe")
    carried = cot_in[0, 0]
    acc_gain = jnp.zeros((2, D), jnp.float32)
    whole_w, whole_g = (
        lax.all_gather(weights, "fsdp", axis=2, tiled=True),
        lax.all_gather(gains, "fsdp", axis=2, tiled=True),
    )
    left_rows = []
    right_first = []
    right_second = []
    for tick in range(TICKS):
        item = (section + tick) % sections
        layer = item % 2 * sections + item - tick
        active = layer >= 0
        stretch = jnp.maximum(layer, 0) // sections
        in_first = active & (stretch == 0)
        in_second = active & (stretch == 1)
        length = lengths[item, 0]
        segment = segments[item, 0]
        gain = whole_g[stretch, 0]
        resid = saved[0, 0, tick].astype(jnp.float32)
        normalized_input, front_pull = jax.vjp(normalize, resid, gain.astype(jnp.float32))
        normed_b = normalized_input.astype(jnp.bfloat16)
        weight = whole_w[stretch, 0]
        key_value_pair = jnp.dot(normed_b, weight, preferred_element_type=jnp.float32)
        direct, normed_cot, keyval_cot = attend_back(
            resid, normalized_input, key_value_pair, carried, length, segment
        )
        normed_total = normed_cot + times_transposed(keyval_cot, weight)
        left_rows.append(normed_b)
        zero_rows = jnp.zeros_like(keyval_cot)
        right_first.append(jnp.where(in_first, keyval_cot, zero_rows))
        right_second.append(jnp.where(in_second, keyval_cot, zero_rows))
        resid_cot, gain_cot = front_pull(normed_total)
        acc_gain = acc_gain.at[stretch].add(jnp.where(active, gain_cot, jnp.zeros_like(gain_cot)))
        carried = jnp.where(active, (direct + resid_cot).astype(jnp.bfloat16), carried)
        if tick + 1 < TICKS:
            carried = passed_along(carried, "pipe", -1)
    normed_all = jnp.concatenate(left_rows, axis=0)
    pair_dims = (((0,), (0,)), ((), ()))
    kv_first = lax.dot_general(
        normed_all,
        jnp.concatenate(right_first, axis=0),
        pair_dims,
        preferred_element_type=jnp.float32,
    )
    kv_second = lax.dot_general(
        normed_all,
        jnp.concatenate(right_second, axis=0),
        pair_dims,
        preferred_element_type=jnp.float32,
    )
    acc_kv = jnp.stack([kv_first, kv_second])
    kv_sum, gain_sum = (
        lax.psum_scatter(
            acc_kv.astype(jnp.bfloat16), "fsdp", scatter_dimension=1, tiled=True
        ).astype(jnp.float32),
        lax.psum_scatter(
            acc_gain.astype(jnp.bfloat16), "fsdp", scatter_dimension=1, tiled=True
        ).astype(jnp.float32),
    )
    grad_kv = kv_sum.astype(jnp.bfloat16)[:, None]
    grad_gain = gain_sum.astype(jnp.bfloat16)[:, None]
    return (carried[None, None], grad_kv, grad_gain)


def solution(mesh):
    in_specs = (
        P("pipe", "fsdp", None, None, None),
        P("pipe", "fsdp", None, None),
        P(None, "pipe", "fsdp", None),
        P(None, "pipe", "fsdp"),
        P(None, "fsdp"),
        P(None, "fsdp", None),
    )
    out_specs = (
        P("pipe", "fsdp", None, None),
        P(None, "pipe", "fsdp", None),
        P(None, "pipe", "fsdp"),
    )
    return jax.shard_map(body, mesh=mesh, in_specs=in_specs, out_specs=out_specs, check_vma=False)
```

profile of v0, /device:TPU:0, one launch (start us, length us, event | category | flops | bytes accessed | tf_op | source)
XLA Modules:
  0.0 687.0 jit_solution(8813813834462477955)
XLA Ops:
  8.2 1.4 constant_dynamic-slice_fusion
  13.9 1.1 convert_bitcast_fusion.11
  15.0 1.2 copy.136
  16.1 1.7 convert_bitcast_fusion.5
  17.8 1.2 copy.143
  19.0 1.2 copy.140
  20.5 28.3 %all_gather.6 = bf16[2,1,4096]{2,0,1:T(2,128)(2,1)S(1)} all-gather(bf16[2,1,512]{2,0,1:T(2,128)(2,1)S(1)} %copy-done.23), channel_id=1, replica_groups=mesh['pipe'=4,'fsdp'=8] {'fsdp'}, dimensions={2}, use_global_device_ids=true | all-gather | bytes 18432 | tf_op jit(solution)/shard_map/all_gather | solution.py:86
  48.8 1.2 fusion.226
  50.0 1.2 fusion.225
  52.2 188.5 %all-gather.2.cloned.1.call-done = bf16[2,1,4096,1024]{3,2,1,0:T(8,128)(2,1)} async-done(((bf16[2,1,512,1024]{3,2,1,0:T(8,128)(2,1)}), bf16[2,1,4096,1024]{3,2,1,0:T(8,128)(2,1)}) %all-gather.2.cloned.1.call-update) | async-done | bytes 16777232 | tf_op jit(solution)/shard_map/all_gather | solution.py:85
  240.7 5.0 fusion.51
  245.8 1.0 fusion.139
  247.1 2.1 fusion.71
  249.2 1.0 fusion.103
  253.1 7.5 %fusion.77 = (f32[4096]{0:T(1024)S(1)}, f32[64]{0:T(128)S(1)}, f32[64]{0:T(128)S(1)}, bf16[64,4096]{1,0:T(8,128)(2,1)}, f32[64,4096]{1,0:T(8,128)S(1)}) fusion(f32[64]{0:T(128)} %copy-done.19, bf16[1,1,3,64,4096]{4,3,2,1,0:T(8,128)(2,1)S(1)} %copy-done, f32[4096]{0:T(1024)S(1)} %bitcast.456, bf16[2,1,4096,1024]{3,2,1,0:T(8,128)(2,1)} %all-gather.2.cloned.1.call-done, ...), kind=kOutput, calls=%fused_computation.109 | convolution fusion | flops 540536704 | bytes 12224000 | tf_op jit(solution)/shard_map/dot_general | solution.py:74
  261.2 5.0 fusion.54
  266.3 1.9 fusion.142
  268.8 2.2 fusion.140
  271.0 1.2 select_select_fusion
  272.2 0.9 scatter-add.10
  274.1 1.7 collective-permute-done
  277.5 1.4 fusion.137
  280.9 1.1 copy.81
  282.1 1.8 copy.82
  283.9 1.4 fusion.69
  285.3 7.8 %fusion.75 = (f32[4096]{0:T(1024)S(1)}, f32[64]{0:T(128)S(1)}, f32[64]{0:T(128)S(1)}, bf16[64,4096]{1,0:T(8,128)(2,1)}, f32[64,4096]{1,0:T(8,128)S(1)}) fusion(f32[64]{0:T(128)} %copy-done.16, bf16[1,1,3,64,4096]{4,3,2,1,0:T(8,128)(2,1)S(1)} %copy-done, f32[4096]{0:T(1024)S(1)} %bitcast.451, bf16[2,1,4096,1024]{3,2,1,0:T(8,128)(2,1)} %all-gather.2.cloned.1.call-done, ...), kind=kOutput, calls=%fused_computation.107 | convolution fusion | flops 540536704 | bytes 12224000 | tf_op jit(solution)/shard_map/dot_general | solution.py:74
  294.2 5.0 fusion.57
  299.3 1.8 fusion.144
  301.1 1.8 collective-permute-start.1
  302.9 1.4 broadcast_select_fusion.7
  304.3 2.2 fusion.141
  307.7 0.9 fusion.163
  308.7 1.3 collective-permute-done.1
  310.9 1.4 fusion.123
  312.4 2.2 fusion.136
  314.5 1.2 fusion.121
  317.1 1.1 copy.92
  318.3 1.8 copy.93
  320.1 1.4 fusion.67
  321.5 7.6 %fusion.73 = (f32[4096]{0:T(1024)S(1)}, f32[64]{0:T(128)S(1)}, bf16[64,4096]{1,0:T(8,128)(2,1)}, f32[64,4096]{1,0:T(8,128)S(1)}) fusion(f32[64]{0:T(128)S(1)} %copy-done.21, bf16[1,1,3,64,4096]{4,3,2,1,0:T(8,128)(2,1)S(1)} %copy-done, f32[4096]{0:T(1024)S(1)} %bitcast.476, bf16[2,1,4096,1024]{3,2,1,0:T(8,128)(2,1)} %all-gather.2.cloned.1.call-done, ...), kind=kOutput, calls=%fused_computation.105 | convolution fusion | flops 539750336 | bytes 11699200 | tf_op jit(solution)/shard_map/dot_general | solution.py:74
  330.0 1.4 copy.128
  331.8 3.7 convert_bitcast_fusion.1
  335.6 2.4 convert_bitcast_fusion
  338.0 6.8 pad_maximum_fusion
  345.9 1.2 fusion.145
  347.0 47.1 %reduce-scatter.7.cloned.1.call-done = bf16[512,2]{1,0:T(8,128)(2,1)} async-done(((bf16[4096,2]{1,0:T(8,128)(2,1)}), bf16[512,2]{1,0:T(8,128)(2,1)}) %reduce-scatter.7.cloned.1.call-update) | async-done | bytes 2064
  394.1 1.6 copy.129
  395.7 284.3 %reduce-scatter.5.cloned.1.call-done = bf16[2,512,1024]{2,1,0:T(8,128)(2,1)} async-done(((bf16[2,4096,1024]{2,1,0:T(8,128)(2,1)}), bf16[2,512,1024]{2,1,0:T(8,128)(2,1)}) %reduce-scatter.5.cloned.1.call-update) | async-done | bytes 2097168 | tf_op jit(solution)/shard_map/reduce_scatter | solution.py:135
  (144 shorter events, 22.2 us)
Async XLA Ops:
  7.2 44.0 %copy-start.30 = (s32[2]{0:T(128)S(1)}, s32[2]{0:T(128)}, u32[]{:S(2)}) copy-start(s32[2]{0:T(128)} %constant.174.clone.1) | copy-start | bytes 28
  7.2 44.8 %copy-start = (bf16[1,1,3,64,4096]{4,3,2,1,0:T(8,128)(2,1)S(1)}, bf16[1,1,3,64,4096]{4,3,2,1,0:T(8,128)(2,1)}, u32[]{:S(2)}) copy-start(bf16[1,1,3,64,4096]{4,3,2,1,0:T(8,128)(2,1)} %param.12) | copy-start | bytes 4718596
  7.2 13.3 %copy-start.23 = (bf16[2,1,512]{2,0,1:T(2,128)(2,1)S(1)}, bf16[2,1,512]{2,0,1:T(2,128)(2,1)}, u32[]{:S(2)}) copy-start(bf16[2,1,512]{2,0,1:T(2,128)(2,1)} %param.15) | copy-start | bytes 6148
  7.2 233.5 %all-gather.2.cloned.1.call-start = ((), (), s32[]{:S(2)}) async-start(), calls=%async_computation.2 | async-start | bytes 18874368 | tf_op jit(solution)/shard_map/all_gather | solution.py:85
  7.9 386.2 %reduce-scatter.7.cloned.1.call-start = ((), (), s32[]{:S(2)}) async-start(), calls=%async_computation.4 | async-start | bytes 1179648
  52.1 197.1 %copy-start.28 = (f32[64]{0:T(128)}, f32[64]{0:T(128)S(1)}, u32[]{:S(2)}) copy-start(f32[64]{0:T(128)S(1)} %fusion.82) | copy-start | bytes 772
  52.2 199.4 %copy-start.19 = (f32[64]{0:T(128)}, f32[64]{0:T(128)S(1)}, u32[]{:S(2)}) copy-start(f32[64]{0:T(128)S(1)} %fusion.213) | copy-start | bytes 772
  245.8 3.4 copy-start.3
  252.6 8.0 %copy-start.29 = (f32[64]{0:T(128)S(1)}, f32[64]{0:T(128)}, u32[]{:S(2)}) copy-start(f32[64]{0:T(128)} %copy-done.28) | copy-start | bytes 772
  253.1 13.2 %copy-start.4 = (bf16[1,1,64,4096]{3,2,1,0:T(8,128)(2,1)S(1)}, bf16[1,1,64,4096]{3,2,1,0:T(8,128)(2,1)}, u32[]{:S(2)}) copy-start(bf16[1,1,64,4096]{3,2,1,0:T(8,128)(2,1)} %param.13) | copy-start | bytes 1572868
  260.6 5.6 copy-start.26
  261.2 5.1 copy-start.16
  268.2 7.7 %collective-permute-start = (bf16[64,4096]{1,0:T(8,128)(2,1)}, bf16[64,4096]{1,0:T(8,128)(2,1)S(1)}, u32[]{:S(2)}, u32[]{:S(2)}) collective-permute-start(bf16[64,4096]{1,0:T(8,128)(2,1)} %fusion.142), channel_id=1, source_target_pairs={{0,24},{8,0},{16,8},{24,16},{1,25},{9,1},{17,9},{25,17},{2,26},{10... | collective-permute-start | bytes 1572872 | tf_op jit(solution)/shard_map/ppermute | solution.py:17
  273.1 6.4 copy-start.2
  273.1 6.4 copy-start.17
  275.8 3.2 copy-start.9
  276.8 2.7 copy-start.6
  280.9 12.7 %copy-start.27 = (f32[64]{0:T(128)S(1)}, f32[64]{0:T(128)}, u32[]{:S(2)}) copy-start(f32[64]{0:T(128)} %copy-done.26) | copy-start | bytes 772
  285.2 14.0 %copy-start.10 = (bf16[64,4096]{1,0:T(8,128)(2,1)S(1)}, bf16[64,4096]{1,0:T(8,128)(2,1)}, u32[]{:S(2)}) copy-start(bf16[64,4096]{1,0:T(8,128)(2,1)} %copy-done.9) | copy-start | bytes 1572868
  285.3 14.0 %copy-start.18 = (f32[64]{0:T(128)S(1)}, f32[64]{0:T(128)}, u32[]{:S(2)}) copy-start(f32[64]{0:T(128)} %copy-done.16) | copy-start | bytes 772
  293.0 6.2 copy-start.24
  293.1 11.3 %copy-start.13 = (pred[64,64]{0,1:T(8,128)(4,1)S(1)}, pred[64,64]{0,1:T(8,128)(4,1)}, u32[]{:S(2)}) copy-start(pred[64,64]{0,1:T(8,128)(4,1)} %copy.87) | copy-start | bytes 12292
  294.2 13.5 %copy-start.20 = (f32[64]{0:T(128)}, f32[64]{0:T(128)S(1)}, u32[]{:S(2)}) copy-start(f32[64]{0:T(128)S(1)} %fusion.215) | copy-start | bytes 772
  301.1 8.8 %collective-permute-start.1 = (bf16[64,4096]{1,0:T(8,128)(2,1)}, bf16[64,4096]{1,0:T(8,128)(2,1)S(1)}, u32[]{:S(2)}, u32[]{:S(2)}) collective-permute-start(bf16[64,4096]{1,0:T(8,128)(2,1)} %fusion.144), channel_id=1, source_target_pairs={{0,24},{8,0},{16,8},{24,16},{1,25},{9,1},{17,9},{25,17},{2,26},{10... | collective-permute-start | bytes 1572872 | tf_op jit(solution)/shard_map/ppermute | solution.py:17
  306.9 8.8 %copy-start.1 = (f32[8,8,32,128]{3,2,1,0:T(8,128)S(1)}, f32[8,8,32,128]{3,2,1,0:T(8,128)}, u32[]{:S(2)}) copy-start(f32[8,8,32,128]{3,2,1,0:T(8,128)} %copy.143) | copy-start | bytes 3145732
  307.7 8.0 %copy-start.21 = (f32[64]{0:T(128)S(1)}, f32[64]{0:T(128)}, u32[]{:S(2)}) copy-start(f32[64]{0:T(128)} %copy-done.20) | copy-start | bytes 772
  310.0 4.6 copy-start.7
  310.9 4.8 copy-start.5
  321.4 10.4 %copy-start.11 = (bf16[64,4096]{1,0:T(8,128)(2,1)S(1)}, bf16[64,4096]{1,0:T(8,128)(2,1)}, u32[]{:S(2)}) copy-start(bf16[64,4096]{1,0:T(8,128)(2,1)} %get-tuple-element.65) | copy-start | bytes 1572868
  329.1 6.5 copy-start.14
  331.5 348.6 %reduce-scatter.5.cloned.1.call-start = ((), (), s32[]{:S(2)}) async-start(), calls=%async_computation.3 | async-start | bytes 18874368 | tf_op jit(solution)/shard_map/reduce_scatter | solution.py:135
  331.8 3.8 copy-start.12
  331.8 3.8 copy-start.15
  331.8 3.8 copy-start.31
  344.8 0.7 copy-start.25
  344.8 1.0 copy-start.8
  344.8 1.0 copy-start.22
Sparse Core Ops, SparseCore 0:
  10.2 230.4 all-gather.1
  331.6 62.5 reduce-scatter.6
  399.0 281.0 reduce-scatter.4
where the time goes:
time: 697 us; the launch traced here: 687 us
  waiting for transfers between devices  524 us (75%)
  matrix products  60.5 us (9%)
  other arithmetic  36.8 us (5%)
  blocking collectives  28.3 us (4%)
  local copies, waits for them, and re-layouts  19.6 us (3%)
  between operations  15.3 us (2%)
    reduce_scatter x1, waiting for transfers between devices, body(): lax.psum_scatter(acc_kv.astype(jnp.bfloat16), 'fsdp', scatter_dimension=1...  284 us
    all_gather x1, waiting for transfers between devices, body(): lax.all_gather(weights, 'fsdp', axis=2, tiled=True)  189 us
    unnamed x4, waiting for transfers between devices  47.8 us
    all_gather x1, blocking collectives, body(): lax.all_gather(gains, 'fsdp', axis=2, tiled=True)  28.3 us
    dot_general x3, matrix products, times_transposed(): lax.dot_general(left, right, (((1,), (1,)), ((), ())), preferred_element_...  22.9 us
    dot_general x3, matrix products, body(): jnp.dot(normed_b, weight, preferred_element_type=jnp.float32)  15 us
  transfers between devices with their start and end apart: 5, of which 5 were waited for; matrix products, arithmetic and copies ran while one was open for 6% of the time, Pallas kernels for 0%

commit v1 on v0

v1 whole, which is shorter than its diff:
```python
import functools

import jax
import jax.numpy as jnp
from jax import lax
from jax.experimental import pallas as pl
from jax.experimental.pallas import tpu as pltpu
from jax.sharding import PartitionSpec as P

HEAD_SIZE = 128
KEY_VALUE_HEADS = 4
TICKS = 3
EPS = 1e-05
MESH = pl.DeviceIdType.MESH
LIMIT = 56 * 1024 * 1024


def passed_along(value, axis, by):
    size = lax.axis_size(axis)
    return lax.ppermute(value, axis, [(i, (i + by) % size) for i in range(size)])


def greet_all(n, me):
    barrier = pltpu.get_barrier_semaphore()

    def greet(k, _):
        pl.semaphore_signal(
            barrier, inc=1, device_id={"fsdp": lax.rem(me + k, n)}, device_id_type=MESH
        )
        return 0

    lax.fori_loop(1, n, greet, 0)
    pl.semaphore_wait(barrier, n - 1)


def to_peer(src, dst, send, recv, peer):
    return pltpu.make_async_remote_copy(
        src_ref=src,
        dst_ref=dst,
        send_sem=send,
        recv_sem=recv,
        device_id={"fsdp": peer},
        device_id_type=MESH,
    )


def stretch_of(section, tick, sections):
    item = lax.rem(section + tick, sections)
    layer = lax.rem(item, 2) * sections + item - tick
    return lax.div(jnp.maximum(layer, 0), sections)


def front_kernel(
    n, sections, saved, w, g, kv, cols, gall, part, ret, xs, xr, gs, gr, ps, pr
):
    me = lax.axis_index("fsdp")
    section = lax.axis_index("pipe")
    width = w.shape[1]
    greet_all(n, me)

    def column_copy(k):
        peer = lax.rem(me + k, n)
        at = pl.ds(pl.multiple_of(peer * width, width), width)
        return to_peer(saved.at[:, :, at], cols.at[k], xs.at[k], xr.at[k], peer)

    def gain_copy(k):
        peer = lax.rem(me + k, n)
        return to_peer(g, gall.at[me], gs.at[k], gr.at[k], peer)

    def back_copy(k):
        peer = lax.rem(me - k + n, n)
        return to_peer(part.at[k], ret.at[k], ps.at[k], pr.at[k], peer)

    def send(k, _):
        column_copy(k).start()
        gain_copy(k).start()
        return 0

    lax.fori_loop(1, n, send, 0)
    gall[me] = g[...]
    cols[0] = saved[:, :, pl.ds(pl.multiple_of(me * width, width), width)]

    def share(k, tick):
        stretch = stretch_of(section, tick, sections)
        gain = g[pl.ds(stretch, 1), :].astype(jnp.float32)
        left = (cols[k, tick].astype(jnp.float32) * gain).astype(jnp.bfloat16)
        return jnp.dot(left, w[stretch], preferred_element_type=jnp.float32)

    for tick in range(TICKS):
        kv[tick] = share(0, tick)

    def answer(k, _):
        column_copy(k).wait_recv()
        for tick in range(TICKS):
            part[k, tick] = share(k, tick).astype(jnp.bfloat16)
        back_copy(k).start()
        return 0

    lax.fori_loop(1, n, answer, 0)

    def collect(k, _):
        back_copy(k).wait_recv()
        kv[...] += ret[k].astype(jnp.float32)
        return 0

    lax.fori_loop(1, n, collect, 0)

    def finish(k, _):
        column_copy(k).wait_send()
        gain_copy(k).wait()
        back_copy(k).wait_send()
        return 0

    lax.fori_loop(1, n, finish, 0)


def front(n, sections, saved, w, g):
    ticks, rows, model = saved.shape
    width, kvw = w.shape[1:]
    vmem = pl.BlockSpec(memory_space=pltpu.VMEM)
    return pl.pallas_call(
        functools.partial(front_kernel, n, sections),
        out_shape=(
            jax.ShapeDtypeStruct((ticks, rows, kvw), jnp.float32),
            jax.ShapeDtypeStruct((n, ticks, rows, width), jnp.bfloat16),
            jax.ShapeDtypeStruct((n, 2, width), jnp.float32),
        ),
        in_specs=[vmem] * 3,
        out_specs=(vmem,) * 3,
        scratch_shapes=[
            pltpu.VMEM((n, ticks, rows, kvw), jnp.bfloat16),
            pltpu.VMEM((n, ticks, rows, kvw), jnp.bfloat16),
        ]
        + [pltpu.SemaphoreType.DMA((n,))] * 6,
        compiler_params=pltpu.CompilerParams(
            collective_id=0, has_side_effects=True, vmem_limit_bytes=LIMIT
        ),
    )(saved, w, g)


def back_kernel(n, sections, tick, kc, w, rows_all, total, part, ks, kr, ps, pr):
    me = lax.axis_index("fsdp")
    section = lax.axis_index("pipe")
    width = w.shape[1]
    stretch = stretch_of(section, tick, sections)
    mine = pl.ds(pl.multiple_of(me * width, width), width)
    greet_all(n, me)

    def row_copy(k):
        return to_peer(kc, rows_all.at[k], ks.at[k], kr.at[k], lax.rem(me + k, n))

    def back_copy(k):
        peer = lax.rem(me - k + n, n)
        return to_peer(part.at[k], total.at[:, mine], ps.at[k], pr.at[k], peer)

    def send(k, _):
        row_copy(k).start()
        return 0

    lax.fori_loop(1, n, send, 0)
    rows_all[0] = kc[...]

    def share(k):
        return lax.dot_general(
            rows_all[k], w[stretch], (((1,), (1,)), ((), ())),
            preferred_element_type=jnp.float32,
        ).astype(jnp.bfloat16)

    total[:, mine] = share(0)

    def answer(k, _):
        row_copy(k).wait_recv()
        part[k] = share(k)
        back_copy(k).start()
        return 0

    lax.fori_loop(1, n, answer, 0)

    def finish(k, _):
        row_copy(k).wait_send()
        back_copy(k).wait()
        return 0

    lax.fori_loop(1, n, finish, 0)


def back(n, sections, tick, kc, w):
    rows, kvw = kc.shape
    width = w.shape[1]
    vmem = pl.BlockSpec(memory_space=pltpu.VMEM)
    return pl.pallas_call(
        functools.partial(back_kernel, n, sections, tick),
        out_shape=(
            jax.ShapeDtypeStruct((n, rows, kvw), jnp.bfloat16),
            jax.ShapeDtypeStruct((rows, n * width), jnp.bfloat16),
        ),
        in_specs=[vmem] * 2,
        out_specs=(vmem,) * 2,
        scratch_shapes=[pltpu.VMEM((n, rows, width), jnp.bfloat16)]
        + [pltpu.SemaphoreType.DMA((n,))] * 4,
        compiler_params=pltpu.CompilerParams(
            collective_id=1 + tick, has_side_effects=True, vmem_limit_bytes=LIMIT
        ),
    )(kc, w)


def gain_kernel(n, sums, out, got, ss, sr):
    me = lax.axis_index("fsdp")
    greet_all(n, me)

    def copy(k):
        peer = lax.rem(me + k, n)
        return to_peer(sums.at[peer], got.at[k], ss.at[k], sr.at[k], peer)

    def send(k, _):
        copy(k).start()
        return 0

    lax.fori_loop(1, n, send, 0)
    out[...] = sums[me]

    def collect(k, _):
        copy(k).wait()
        out[...] += got[k]
        return 0

    lax.fori_loop(1, n, collect, 0)


def gain_sums(n, sums):
    vmem = pl.BlockSpec(memory_space=pltpu.VMEM)
    return pl.pallas_call(
        functools.partial(gain_kernel, n),
        out_shape=jax.ShapeDtypeStruct(sums.shape[1:], jnp.float32),
        in_specs=[vmem],
        out_specs=vmem,
        scratch_shapes=[pltpu.VMEM(sums.shape, jnp.float32)]
        + [pltpu.SemaphoreType.DMA((n,))] * 2,
        compiler_params=pltpu.CompilerParams(
            collective_id=1 + TICKS, has_side_effects=True, vmem_limit_bytes=LIMIT
        ),
    )(sums)


def normalize(resid, gain):
    factor = lax.rsqrt(jnp.mean(resid * resid, axis=-1, keepdims=True) + EPS)
    return resid * factor * gain


def attend(resid, normalized_input, key_value_pair, length, segment):
    item_count = resid.shape[0]
    model_width = resid.shape[1]
    query_groups = model_width // HEAD_SIZE // KEY_VALUE_HEADS
    query_rows = normalized_input.astype(jnp.bfloat16).reshape(
        item_count, KEY_VALUE_HEADS, query_groups, HEAD_SIZE
    )
    key_rows = (
        key_value_pair[:, : KEY_VALUE_HEADS * HEAD_SIZE]
        .astype(jnp.bfloat16)
        .reshape(item_count, KEY_VALUE_HEADS, HEAD_SIZE)
    )
    value_rows = (
        key_value_pair[:, KEY_VALUE_HEADS * HEAD_SIZE :]
        .astype(jnp.bfloat16)
        .reshape(item_count, KEY_VALUE_HEADS, HEAD_SIZE)
    )
    scores = jnp.einsum(
        "pkgd,qkd->kgpq", query_rows, key_rows, preferred_element_type=jnp.float32
    ) * HEAD_SIZE ** (-0.5)
    place = jnp.arange(item_count, dtype=jnp.int32)
    allowed = (
        (segment[:, None] == segment[None, :])
        & (place[None, :] <= place[:, None])
        & (place[None, :] < length)
    )
    allowed = allowed | (place[:, None] == place[None, :])
    scores = jnp.where(allowed, scores, -1e30)
    peak = jnp.max(scores, axis=-1, keepdims=True)
    expo = jnp.exp(scores - peak)
    probs = (expo / jnp.sum(expo, axis=-1, keepdims=True)).astype(jnp.bfloat16)
    mixed = jnp.einsum(
        "kgpq,qkd->pkgd", probs, value_rows, preferred_element_type=jnp.float32
    ).reshape(item_count, model_width)
    valid = (place < length).astype(jnp.float32)
    return resid + mixed * valid[:, None]


def body(saved, cot_in, weights, gains, lengths, segments):
    sections = lax.axis_size("pipe")
    n = lax.axis_size("fsdp")
    section = lax.axis_index("pipe")
    carried = cot_in[0, 0]
    model = carried.shape[-1]
    w, g = weights[:, 0], gains[:, 0]
    own_gain = g.astype(jnp.float32)
    kv, cols, gall = front(n, sections, saved[0, 0], w, own_gain)
    whole_g = jnp.swapaxes(gall, 0, 1).reshape(2, model)
    acc_gain = jnp.zeros((2, model), jnp.float32)
    right = []
    for tick in range(TICKS):
        item = (section + tick) % sections
        layer = item % 2 * sections + item - tick
        active = layer >= 0
        stretch = jnp.maximum(layer, 0) // sections
        length = lengths[item, 0]
        segment = segments[item, 0]
        resid = saved[0, 0, tick].astype(jnp.float32)
        factor = lax.rsqrt(jnp.mean(resid * resid, axis=-1, keepdims=True) + EPS)
        normalized_input, front_pull = jax.vjp(normalize, resid, whole_g[stretch])

        def inner(first, second, third):
            return attend(first, second, third, length, segment)

        _, pull = jax.vjp(inner, resid, normalized_input, kv[tick] * factor)
        direct, normed_cot, keyval_cot = pull(carried.astype(jnp.float32))
        scaled = jnp.where(active, keyval_cot * factor, 0.0).astype(jnp.bfloat16)
        rows_all, product = back(n, sections, tick, scaled, w)
        right.append((rows_all, active & (stretch == 0), active & (stretch == 1)))
        normed_total = normed_cot + product.astype(jnp.float32) / factor
        resid_cot, gain_cot = front_pull(normed_total)
        acc_gain = acc_gain.at[stretch].add(jnp.where(active, gain_cot, 0.0))
        carried = jnp.where(active, (direct + resid_cot).astype(jnp.bfloat16), carried)
        if tick + 1 < TICKS:
            carried = passed_along(carried, "pipe", -1)
    width = w.shape[1]
    sums = jnp.swapaxes(acc_gain.reshape(2, n, width), 0, 1)
    grad_gain = gain_sums(n, sums).astype(jnp.bfloat16)[:, None]
    left = cols.reshape(-1, width)
    grads = []
    for which in (1, 2):
        block = jnp.stack(
            [jnp.where(r[which], r[0], jnp.zeros_like(r[0])) for r in right], axis=1
        ).reshape(left.shape[0], -1)
        grads.append(
            lax.dot_general(
                left, block, (((0,), (0,)), ((), ())), preferred_element_type=jnp.float32
            )
        )
    grad_kv = (jnp.stack(grads) * own_gain[:, :, None]).astype(jnp.bfloat16)[:, None]
    return (carried[None, None], grad_kv, grad_gain)


def solution(mesh):
    in_specs = (
        P("pipe", "fsdp", None, None, None),
        P("pipe", "fsdp", None, None),
        P(None, "pipe", "fsdp", None),
        P(None, "pipe", "fsdp"),
        P(None, "fsdp"),
        P(None, "fsdp", None),
    )
    out_specs = (
        P("pipe", "fsdp", None, None),
        P(None, "pipe", "fsdp", None),
        P(None, "pipe", "fsdp"),
    )
    return jax.shard_map(body, mesh=mesh, in_specs=in_specs, out_specs=out_specs, check_vma=False)
```

time: 697 us -> 329 us (0.47); the launches traced: 687 us -> 328 us
  waiting for transfers between devices: 524 us -> 3.99 us
  Pallas kernels: 0 us -> 253 us
  matrix products: 60.5 us -> 18 us
  blocking collectives: 28.3 us -> 0 us
  between operations: 15.3 us -> 1.77 us
  local copies, waits for them, and re-layouts: 19.6 us -> 9.06 us
    reduce_scatter x1 -> x0, waiting for transfers between devices: 284 us -> none  [body(): lax.psum_scatter(acc_kv.astype(jnp.bfloat16), 'fsdp', scatter_dimension=1...]
    pallas_call x0 -> x5, Pallas kernels: none -> 253 us  [the longest x1 126 us: front(): pl.pallas_call(functools.partial(front_kernel, n, sections), out_shape=(j...]
    all_gather x1 -> x0, waiting for transfers between devices: 189 us -> none  [body(): lax.all_gather(weights, 'fsdp', axis=2, tiled=True)]
    unnamed x4 -> x0, waiting for transfers between devices: 47.8 us -> none
    dot_general x8 -> x2, matrix products: 44.1 us -> 5.17 us  [body(): lax.dot_general(left, block, (((0,), (0,)), ((), ())), preferred_element_...]
    all_gather x1 -> x0, blocking collectives: 28.3 us -> none  [body(): lax.all_gather(gains, 'fsdp', axis=2, tiled=True)]
    reduce_sum x1 -> x4, other arithmetic: 0.21 us -> 7.95 us  [the longest x3 6.7 us: normalize(): return resid * factor * gain]
  transfers between devices with their start and end apart: 5 -> 2, of which waited for: 5 -> 1; matrix products, arithmetic and copies ran while one was open for 6% -> 5% of each run, Pallas kernels for 0% -> 0%
where the time goes in v1:
time: 329 us; the launch traced here: 328 us
  Pallas kernels  253 us (77%)
  other arithmetic  41.5 us (13%)
  matrix products  18 us (5%)
  local copies, waits for them, and re-layouts  9.06 us (3%)
  waiting for transfers between devices  3.99 us (1%)
    pallas_call x1, Pallas kernels, front(): pl.pallas_call(functools.partial(front_kernel, n, sections), out_shape=(j...  126 us
    pallas_call x3, Pallas kernels, back(): pl.pallas_call(functools.partial(back_kernel, n, sections, tick), out_sha...  120 us
    dot_general x9, matrix products, attend(): jnp.einsum('pkgd,qkd->kgpq', query_rows, key_rows, preferred_element_type...  8.35 us
    pallas_call x1, Pallas kernels, gain_sums(): pl.pallas_call(functools.partial(gain_kernel, n), out_shape=jax.ShapeDtyp...  7.89 us
    reduce_sum x3, other arithmetic, normalize(): return resid * factor * gain  6.7 us
  transfers between devices with their start and end apart: 2, of which 1 were waited for; matrix products, arithmetic and copies ran while one was open for 5% of the time, Pallas kernels for 0%

profile of v1, /device:TPU:0, one launch (start us, length us, event | category | flops | bytes accessed | tf_op | source)
XLA Modules:
  0.0 328.0 jit_solution(16887024816914129432)
XLA Ops:
  0.8 1.2 fusion.45
  2.1 3.1 convert_bitcast_fusion.3
  7.5 125.7 %shard_map.85 = (f32[3,64,1024]{2,1,0:T(8,128)}, bf16[8,3,64,512]{3,2,1,0:T(8,128)(2,1)}, f32[8,2,512]{2,1,0:T(2,128)}) custom-call(bf16[3,64,4096]{2,1,0:T(8,128)(2,1)} %bitcast.445, bf16[2,512,1024]{2,1,0:T(8,128)(2,1)} %bitcast.446, f32[2,512]{1,0:T(2,128)} %bitcast_convert_fusion.g), custom_call_target="tpu_custom_call" | custom-call | tf_op jit(solution)/shard_map/pallas_call | solution.py:121
  133.2 1.0 fusion.125
  134.6 1.0 fusion.108
  135.8 0.9 fusion.40
  136.8 1.0 fusion.66
  137.8 0.7 fusion.103
  139.0 0.8 fusion.39
  140.6 0.8 select_convert_fusion.2.kc
  141.4 31.3 %shard_map.86 = (bf16[8,64,1024]{2,1,0:T(8,128)(2,1)}, bf16[64,4096]{1,0:T(8,128)(2,1)}) custom-call(bf16[64,1024]{1,0:T(8,128)(2,1)} %select_convert_fusion.2.kc, bf16[2,512,1024]{2,1,0:T(8,128)(2,1)} %bitcast.447), custom_call_target="tpu_custom_call" | custom-call | tf_op jit(solution)/shard_map/pallas_call | solution.py:191
  172.7 2.3 fusion.48
  175.0 1.8 fusion.111
  177.5 0.7 iota_compare_fusion.4
  179.8 1.4 copy.89
  181.2 2.4 copy.86
  183.6 1.0 fusion.124
  184.7 0.8 and_reduce_fusion
  185.6 0.7 select_select_fusion
  186.6 2.3 fusion.109
  189.2 1.5 select_bitcast_fusion.5
  191.5 0.7 fusion.76
  192.2 0.7 fusion.102
  193.5 0.8 fusion.37
  194.2 1.1 copy.24
  195.3 1.3 fusion.26
  196.8 0.9 select_convert_fusion.1.kc
  197.7 44.2 %shard_map.87 = (bf16[8,64,1024]{2,1,0:T(8,128)(2,1)}, bf16[64,4096]{1,0:T(8,128)(2,1)}) custom-call(bf16[64,1024]{1,0:T(8,128)(2,1)} %select_convert_fusion.1.kc, bf16[2,512,1024]{2,1,0:T(8,128)(2,1)} %bitcast.448), custom_call_target="tpu_custom_call" | custom-call | tf_op jit(solution)/shard_map/pallas_call | solution.py:191
  242.0 2.3 fusion.52
  245.1 1.0 fusion.123
  246.3 2.4 fusion.113
  249.0 1.0 fusion.110
  250.3 1.4 select_bitcast_fusion.4
  251.7 4.0 %collective-permute-done.1 = bf16[64,4096]{1,0:T(8,128)(2,1)S(1)} collective-permute-done((bf16[64,4096]{1,0:T(8,128)(2,1)S(1)}, bf16[64,4096]{1,0:T(8,128)(2,1)S(1)}, u32[]{:S(2)}, u32[]{:S(2)}) %collective-permute-start.1) | collective-permute-done | bytes 524320 | tf_op jit(solution)/shard_map/ppermute | solution.py:20
  256.5 0.7 fusion.86
  257.3 0.7 fusion.101
  258.5 0.8 fusion.35
  260.0 0.7 select_convert_fusion.kc
  260.8 44.3 %shard_map.88 = (bf16[8,64,1024]{2,1,0:T(8,128)(2,1)}, bf16[64,4096]{1,0:T(8,128)(2,1)}) custom-call(bf16[64,1024]{1,0:T(8,128)(2,1)} %select_convert_fusion.kc, bf16[2,512,1024]{2,1,0:T(8,128)(2,1)} %bitcast.449), custom_call_target="tpu_custom_call" | custom-call | tf_op jit(solution)/shard_map/pallas_call | solution.py:191
  305.1 2.1 fusion.56
  307.2 0.7 broadcast_select_fusion
  308.7 7.9 %shard_map.89 = f32[2,512]{1,0:T(2,128)} custom-call(f32[8,2,512]{2,1,0:T(2,128)} %bitcast.487), custom_call_target="tpu_custom_call" | custom-call | tf_op jit(solution)/shard_map/pallas_call | solution.py:232
  316.6 1.3 convert_bitcast_fusion.10
  317.8 1.4 select_bitcast_fusion.3
  319.3 3.4 %fusion.5 = f32[1,1,512,1024]{3,2,1,0:T(8,128)S(1)} fusion(bf16[8,3,64,512]{3,2,1,0:T(8,128)(2,1)} %get-tuple-element.53, bf16[8,1,64,1024]{3,2,0,1:T(8,128)(2,1)S(1)} %get-tuple-element.81, bf16[8,1,64,1024]{3,2,0,1:T(8,128)(2,1)S(1)} %copy-done.15, bf16[8,1,64,1024]{3,2,0,1:T(8,128)(2,1)S(1)} %copy-done.12), kind=kOutput, calls=%fused_computation.8 | convolution fusion | flops 1613758464 | bytes 6815744 | tf_op jit(solution)/shard_map/dot_general | solution.py:335
  322.7 1.8 fusion.8
  324.5 1.6 fusion
  326.1 1.8 fusion.114
  (125 shorter events, 13.0 us)
Async XLA Ops:
  2.0 3.1 copy-start.20
  2.0 3.7 %copy-start.22 = (s32[4,1,64]{2,1,0:T(1,128)S(1)}, s32[4,1,64]{2,1,0:T(1,128)}, u32[]{:S(2)}) copy-start(s32[4,1,64]{2,1,0:T(1,128)} %param.17) | copy-start | bytes 3076
  2.0 4.4 %copy-start.21 = (bf16[2,1,512]{2,0,1:T(2,128)(2,1)S(1)}, bf16[2,1,512]{2,0,1:T(2,128)(2,1)}, u32[]{:S(2)}) copy-start(bf16[2,1,512]{2,0,1:T(2,128)(2,1)} %param.15) | copy-start | bytes 6148
  2.1 5.2 %copy-start.3 = (bf16[1,1,64,4096]{3,2,1,0:T(8,128)(2,1)S(1)}, bf16[1,1,64,4096]{3,2,1,0:T(8,128)(2,1)}, u32[]{:S(2)}) copy-start(bf16[1,1,64,4096]{3,2,1,0:T(8,128)(2,1)} %param.13) | copy-start | bytes 1572868
  133.2 1.3 copy-start.18
  140.5 32.2 %copy-start = (bf16[1,1,3,64,4096]{4,3,2,1,0:T(8,128)(2,1)S(1)}, bf16[1,1,3,64,4096]{4,3,2,1,0:T(8,128)(2,1)}, u32[]{:S(2)}) copy-start(bf16[1,1,3,64,4096]{4,3,2,1,0:T(8,128)(2,1)} %param.12) | copy-start | bytes 4718596
  141.4 33.6 %copy-start.4 = (bf16[1,1,64,4096]{3,2,1,0:T(8,128)(2,1)S(1)}, bf16[1,1,64,4096]{3,2,1,0:T(8,128)(2,1)}, u32[]{:S(2)}) copy-start(bf16[1,1,64,4096]{3,2,1,0:T(8,128)(2,1)} %param.13) | copy-start | bytes 1572868
  172.7 2.3 copy-start.10
  176.9 13.8 %collective-permute-start = (bf16[64,4096]{1,0:T(8,128)(2,1)}, bf16[64,4096]{1,0:T(8,128)(2,1)S(1)}, u32[]{:S(2)}, u32[]{:S(2)}) collective-permute-start(bf16[64,4096]{1,0:T(8,128)(2,1)} %fusion.111), channel_id=1, source_target_pairs={{0,24},{8,0},{16,8},{24,16},{1,25},{9,1},{17,9},{25,17},{2,26},{10... | collective-permute-start | bytes 1572872 | tf_op jit(solution)/shard_map/ppermute | solution.py:20
  179.8 4.9 %copy-start.23 = (s32[2]{0:T(128)S(1)}, s32[2]{0:T(128)}, u32[]{:S(2)}) copy-start(s32[2]{0:T(128)} %constant.173.clone.1) | copy-start | bytes 28
  186.6 2.6 copy-start.13
  190.6 0.8 copy-start.5
  192.2 1.2 copy-start.1
  196.8 47.5 %copy-start.2 = (f32[64,4,8,128]{3,2,1,0:T(8,128)}, f32[64,4,8,128]{3,2,1,0:T(8,128)S(1)}, u32[]{:S(2)}) copy-start(f32[64,4,8,128]{3,2,1,0:T(8,128)S(1)} %copy.26) | copy-start | bytes 3145732
  242.0 4.3 %copy-start.6 = (bf16[64,4096]{1,0:T(8,128)(2,1)S(1)}, bf16[64,4096]{1,0:T(8,128)(2,1)}, u32[]{:S(2)}) copy-start(bf16[64,4096]{1,0:T(8,128)(2,1)} %copy-done.5) | copy-start | bytes 1572868
  248.7 1.5 copy-start.16
  248.7 7.0 %collective-permute-start.1 = (bf16[64,4096]{1,0:T(8,128)(2,1)S(1)}, bf16[64,4096]{1,0:T(8,128)(2,1)S(1)}, u32[]{:S(2)}, u32[]{:S(2)}) collective-permute-start(bf16[64,4096]{1,0:T(8,128)(2,1)S(1)} %fusion.113), channel_id=1, source_target_pairs={{0,24},{8,0},{16,8},{24,16},{1,25},{9,1},{17,9},{25,17},{2,26},{10... | collective-permute-start | bytes 1572872 | tf_op jit(solution)/shard_map/ppermute | solution.py:20
  255.7 0.8 copy-start.7
  308.1 0.6 copy-start.17
  308.1 11.1 %copy-start.12 = (bf16[8,1,64,1024]{3,2,0,1:T(8,128)(2,1)S(1)}, bf16[8,1,64,1024]{3,2,0,1:T(8,128)(2,1)}, u32[]{:S(2)}) copy-start(bf16[8,1,64,1024]{3,2,0,1:T(8,128)(2,1)} %get-tuple-element.77) | copy-start | bytes 3145732
  308.1 11.1 %copy-start.15 = (bf16[8,1,64,1024]{3,2,0,1:T(8,128)(2,1)S(1)}, bf16[8,1,64,1024]{3,2,0,1:T(8,128)(2,1)}, u32[]{:S(2)}) copy-start(bf16[8,1,64,1024]{3,2,0,1:T(8,128)(2,1)} %get-tuple-element.79) | copy-start | bytes 3145732
  319.2 3.4 %copy-start.11 = (bf16[8,1,64,1024]{3,2,0,1:T(8,128)(2,1)S(1)}, bf16[8,1,64,1024]{3,2,0,1:T(8,128)(2,1)}, u32[]{:S(2)}) copy-start(bf16[8,1,64,1024]{3,2,0,1:T(8,128)(2,1)} %get-tuple-element.78) | copy-start | bytes 3145732
  319.2 3.4 %copy-start.14 = (bf16[8,1,64,1024]{3,2,0,1:T(8,128)(2,1)S(1)}, bf16[8,1,64,1024]{3,2,0,1:T(8,128)(2,1)}, u32[]{:S(2)}) copy-start(bf16[8,1,64,1024]{3,2,0,1:T(8,128)(2,1)} %get-tuple-element.80) | copy-start | bytes 3145732
  319.3 3.4 %copy-start.24 = (bf16[8,3,64,512]{3,2,1,0:T(8,128)(2,1)S(1)}, bf16[8,3,64,512]{3,2,1,0:T(8,128)(2,1)}, u32[]{:S(2)}) copy-start(bf16[8,3,64,512]{3,2,1,0:T(8,128)(2,1)} %get-tuple-element.53) | copy-start | bytes 4718596
  322.7 1.8 copy-start.19
  324.5 1.6 copy-start.8
  324.5 1.6 copy-start.9

commit v2 on v1

--- a/solution.py
+++ b/solution.py
@@ -51,118 +51,216 @@
 
 
 def front_kernel(
-    n, sections, saved, w, g, kv, cols, gall, part, ret, xs, xr, gs, gr, ps, pr
+    n, sections, saved, w, g, kv, cols, gall, w2,
+    pair_g, wide, part, ret, xs, xr, fs, fr, ps, pr, gs, gr, ws, wr, qs, qr
 ):
     me = lax.axis_index("fsdp")
     section = lax.axis_index("pipe")
     width = w.shape[1]
+    steps = n // 2
+    place, half = lax.div(me, 2), lax.rem(me, 2)
+    buddy = place * 2 + 1 - half
+    first = stretch_of(section, 0, sections)
+    second = 1 - first
+    late = stretch_of(section, 2, sections)
+    own_rows = pl.ds(pl.multiple_of(half * width, width), width)
+    buddy_rows = pl.ds(pl.multiple_of((1 - half) * width, width), width)
     greet_all(n, me)
 
-    def column_copy(k):
-        peer = lax.rem(me + k, n)
-        at = pl.ds(pl.multiple_of(peer * width, width), width)
-        return to_peer(saved.at[:, :, at], cols.at[k], xs.at[k], xr.at[k], peer)
+    def weight_copy(i, stretch):
+        return to_peer(w.at[stretch], w2.at[stretch, own_rows], ws.at[i], wr.at[i], buddy)
+
+    def pair_gain_copy():
+        return to_peer(g, pair_g.at[half], qs, qr, buddy)
+
+    def column_copy(k, tick):
+        to = lax.rem(place + k, steps)
+        at = pl.ds(pl.multiple_of(to * 2 * width, 2 * width), 2 * width)
+        return to_peer(
+            saved.at[tick, :, at], wide.at[k, tick], xs.at[k, tick], xr.at[k, tick],
+            to * 2 + half,
+        )
+
+    def half_copy(k, tick):
+        return to_peer(
+            wide.at[k, tick, :, buddy_rows], cols.at[1, k, tick],
+            fs.at[k, tick], fr.at[k, tick], buddy,
+        )
 
     def gain_copy(k):
         peer = lax.rem(me + k, n)
         return to_peer(g, gall.at[me], gs.at[k], gr.at[k], peer)
 
-    def back_copy(k):
-        peer = lax.rem(me - k + n, n)
-        return to_peer(part.at[k], ret.at[k], ps.at[k], pr.at[k], peer)
-
-    def send(k, _):
-        column_copy(k).start()
+    def back_copy(k, tick):
+        to = lax.rem(place - k + steps, steps)
+        return to_peer(
+            part.at[k, tick], ret.at[k, tick], ps.at[k, tick], pr.at[k, tick],
+            to * 2 + half,
+        )
+
+    pair_gain_copy().start()
+    weight_copy(0, first).start()
+    for tick in (0, 2, 1):
+
+        def send(k, _, tick=tick):
+            column_copy(k, tick).start()
+            return 0
+
+        lax.fori_loop(1, steps, send, 0)
+    weight_copy(1, second).start()
+
+    def send_gain(k, _):
         gain_copy(k).start()
         return 0
 
-    lax.fori_loop(1, n, send, 0)
+    lax.fori_loop(1, n, send_gain, 0)
     gall[me] = g[...]
-    cols[0] = saved[:, :, pl.ds(pl.multiple_of(me * width, width), width)]
+    pair_g[half] = g[...]
+    at = pl.ds(pl.multiple_of(place * 2 * width, 2 * width), 2 * width)
+    wide[0] = saved[:, :, at]
+    w2[:, own_rows, :] = w[...]
+    for tick in (0, 2, 1):
+        half_copy(0, tick).start()
+    pair_gain_copy().wait_recv()
 
     def share(k, tick):
         stretch = stretch_of(section, tick, sections)
-        gain = g[pl.ds(stretch, 1), :].astype(jnp.float32)
-        left = (cols[k, tick].astype(jnp.float32) * gain).astype(jnp.bfloat16)
-        return jnp.dot(left, w[stretch], preferred_element_type=jnp.float32)
-
-    for tick in range(TICKS):
+        total = None
+        for side in range(2):
+            at = pl.ds(side * width, width)
+            gain = pair_g[side, pl.ds(stretch, 1), :]
+            left = (wide[k, tick, :, at].astype(jnp.float32) * gain).astype(jnp.bfloat16)
+            term = jnp.dot(left, w2[stretch, at, :], preferred_element_type=jnp.float32)
+            total = term if total is None else total + term
+        return total
+
+    weight_copy(0, first).wait_recv()
+    for tick in (0, 2, 1):
+        if tick == 2:
+
+            @pl.when(late != first)
+            def _():
+                weight_copy(1, second).wait_recv()
+
+        if tick == 1:
+
+            @pl.when(late == first)
+            def _():
+                weight_copy(1, second).wait_recv()
+
+        def answer(k, _, tick=tick):
+            column_copy(k, tick).wait_recv()
+            half_copy(k, tick).start()
+            part[k, tick] = share(k, tick).astype(jnp.bfloat16)
+            back_copy(k, tick).start()
+            return 0
+
+        lax.fori_loop(1, steps, answer, 0)
         kv[tick] = share(0, tick)
 
-    def answer(k, _):
-        column_copy(k).wait_recv()
-        for tick in range(TICKS):
-            part[k, tick] = share(k, tick).astype(jnp.bfloat16)
-        back_copy(k).start()
-        return 0
-
-    lax.fori_loop(1, n, answer, 0)
-
-    def collect(k, _):
-        back_copy(k).wait_recv()
-        kv[...] += ret[k].astype(jnp.float32)
-        return 0
-
-    lax.fori_loop(1, n, collect, 0)
-
-    def finish(k, _):
-        column_copy(k).wait_send()
+    def own_half(k, _):
+        cols[0, k] = wide[k, :, :, own_rows]
+        return 0
+
+    lax.fori_loop(0, steps, own_half, 0)
+    for tick in (0, 2, 1):
+
+        def collect(k, _, tick=tick):
+            back_copy(k, tick).wait_recv()
+            kv[tick] += ret[k, tick].astype(jnp.float32)
+            return 0
+
+        lax.fori_loop(1, steps, collect, 0)
+        half_copy(0, tick).wait()
+
+        def finish(k, _, tick=tick):
+            column_copy(k, tick).wait_send()
+            half_copy(k, tick).wait()
+            back_copy(k, tick).wait_send()
+            return 0
+
+        lax.fori_loop(1, steps, finish, 0)
+
+    def finish_gain(k, _):
         gain_copy(k).wait()
-        back_copy(k).wait_send()
-        return 0
-
-    lax.fori_loop(1, n, finish, 0)
+        return 0
+
+    lax.fori_loop(1, n, finish_gain, 0)
+    pair_gain_copy().wait_send()
+    weight_copy(0, first).wait_send()
+    weight_copy(1, second).wait_send()
 
 
 def front(n, sections, saved, w, g):
     ticks, rows, model = saved.shape
     width, kvw = w.shape[1:]
+    steps = n // 2
     vmem = pl.BlockSpec(memory_space=pltpu.VMEM)
+    dma = pltpu.SemaphoreType.DMA
     return pl.pallas_call(
         functools.partial(front_kernel, n, sections),
         out_shape=(
             jax.ShapeDtypeStruct((ticks, rows, kvw), jnp.float32),
-            jax.ShapeDtypeStruct((n, ticks, rows, width), jnp.bfloat16),
+            jax.ShapeDtypeStruct((2, steps, ticks, rows, width), jnp.bfloat16),
             jax.ShapeDtypeStruct((n, 2, width), jnp.float32),
+            jax.ShapeDtypeStruct((2, 2 * width, kvw), jnp.bfloat16),
         ),
         in_specs=[vmem] * 3,
-        out_specs=(vmem,) * 3,
+        out_specs=(vmem,) * 4,
         scratch_shapes=[
-            pltpu.VMEM((n, ticks, rows, kvw), jnp.bfloat16),
-            pltpu.VMEM((n, ticks, rows, kvw), jnp.bfloat16),
+            pltpu.VMEM((2, 2, width), jnp.float32),
+            pltpu.VMEM((steps, ticks, rows, 2 * width), jnp.bfloat16),
+            pltpu.VMEM((steps, ticks, rows, kvw), jnp.bfloat16),
+            pltpu.VMEM((steps, ticks, rows, kvw), jnp.bfloat16),
         ]
-        + [pltpu.SemaphoreType.DMA((n,))] * 6,
+        + [dma((steps, ticks))] * 6
+        + [dma((n,))] * 2
+        + [dma((2,))] * 2
+        + [dma] * 2,
         compiler_params=pltpu.CompilerParams(
             collective_id=0, has_side_effects=True, vmem_limit_bytes=LIMIT
         ),
     )(saved, w, g)
 
 
-def back_kernel(n, sections, tick, kc, w, rows_all, total, part, ks, kr, ps, pr):
+def back_kernel(
+    n, sections, tick, kc, w2, rows_all, total, part, ks, kr, fs, fr, ps, pr
+):
     me = lax.axis_index("fsdp")
     section = lax.axis_index("pipe")
-    width = w.shape[1]
+    wide = w2.shape[1]
+    steps = n // 2
+    place, half = lax.div(me, 2), lax.rem(me, 2)
+    buddy = place * 2 + 1 - half
     stretch = stretch_of(section, tick, sections)
-    mine = pl.ds(pl.multiple_of(me * width, width), width)
+    mine = pl.ds(pl.multiple_of(place * wide, wide), wide)
     greet_all(n, me)
 
     def row_copy(k):
-        return to_peer(kc, rows_all.at[k], ks.at[k], kr.at[k], lax.rem(me + k, n))
+        to = lax.rem(place + k, steps) * 2 + half
+        return to_peer(kc, rows_all.at[0, k], ks.at[k], kr.at[k], to)
+
+    def own_copy():
+        return to_peer(kc, rows_all.at[1, 0], fs.at[0], fr.at[0], buddy)
+
+    def pair_copy(k):
+        return to_peer(rows_all.at[0, k], rows_all.at[1, k], fs.at[k], fr.at[k], buddy)
 
     def back_copy(k):
-        peer = lax.rem(me - k + n, n)
-        return to_peer(part.at[k], total.at[:, mine], ps.at[k], pr.at[k], peer)
+        to = lax.rem(place - k + steps, steps) * 2 + half
+        return to_peer(part.at[k], total.at[:, mine], ps.at[k], pr.at[k], to)
 
     def send(k, _):
         row_copy(k).start()
         return 0
 
-    lax.fori_loop(1, n, send, 0)
-    rows_all[0] = kc[...]
+    lax.fori_loop(1, steps, send, 0)
+    own_copy().start()
+    rows_all[0, 0] = kc[...]
 
     def share(k):
         return lax.dot_general(
-            rows_all[k], w[stretch], (((1,), (1,)), ((), ())),
+            rows_all[0, k], w2[stretch], (((1,), (1,)), ((), ())),
             preferred_element_type=jnp.float32,
         ).astype(jnp.bfloat16)
 
@@ -170,38 +268,42 @@
 
     def answer(k, _):
         row_copy(k).wait_recv()
+        pair_copy(k).start()
         part[k] = share(k)
         back_copy(k).start()
         return 0
 
-    lax.fori_loop(1, n, answer, 0)
+    lax.fori_loop(1, steps, answer, 0)
+    own_copy().wait()
 
     def finish(k, _):
         row_copy(k).wait_send()
+        pair_copy(k).wait()
         back_copy(k).wait()
         return 0
 
-    lax.fori_loop(1, n, finish, 0)
-
-
-def back(n, sections, tick, kc, w):
+    lax.fori_loop(1, steps, finish, 0)
+
+
+def back(n, sections, tick, kc, w2):
     rows, kvw = kc.shape
-    width = w.shape[1]
+    wide = w2.shape[1]
+    steps = n // 2
     vmem = pl.BlockSpec(memory_space=pltpu.VMEM)
     return pl.pallas_call(
         functools.partial(back_kernel, n, sections, tick),
         out_shape=(
-            jax.ShapeDtypeStruct((n, rows, kvw), jnp.bfloat16),
-            jax.ShapeDtypeStruct((rows, n * width), jnp.bfloat16),
+            jax.ShapeDtypeStruct((2, steps, rows, kvw), jnp.bfloat16),
+            jax.ShapeDtypeStruct((rows, steps * wide), jnp.bfloat16),
         ),
         in_specs=[vmem] * 2,
         out_specs=(vmem,) * 2,
-        scratch_shapes=[pltpu.VMEM((n, rows, width), jnp.bfloat16)]
-        + [pltpu.SemaphoreType.DMA((n,))] * 4,
+        scratch_shapes=[pltpu.VMEM((steps, rows, wide), jnp.bfloat16)]
+        + [pltpu.SemaphoreType.DMA((steps,))] * 6,
         compiler_params=pltpu.CompilerParams(
             collective_id=1 + tick, has_side_effects=True, vmem_limit_bytes=LIMIT
         ),
-    )(kc, w)
+    )(kc, w2)
 
 
 def gain_kernel(n, sums, out, got, ss, sr):
@@ -293,7 +395,7 @@
     model = carried.shape[-1]
     w, g = weights[:, 0], gains[:, 0]
     own_gain = g.astype(jnp.float32)
-    kv, cols, gall = front(n, sections, saved[0, 0], w, own_gain)
+    kv, cols, gall, w2 = front(n, sections, saved[0, 0], w, own_gain)
     whole_g = jnp.swapaxes(gall, 0, 1).reshape(2, model)
     acc_gain = jnp.zeros((2, model), jnp.float32)
     right = []
@@ -314,7 +416,7 @@
         _, pull = jax.vjp(inner, resid, normalized_input, kv[tick] * factor)
         direct, normed_cot, keyval_cot = pull(carried.astype(jnp.float32))
         scaled = jnp.where(active, keyval_cot * factor, 0.0).astype(jnp.bfloat16)
-        rows_all, product = back(n, sections, tick, scaled, w)
+        rows_all, product = back(n, sections, tick, scaled, w2)
         right.append((rows_all, active & (stretch == 0), active & (stretch == 1)))
         normed_total = normed_cot + product.astype(jnp.float32) / factor
         resid_cot, gain_cot = front_pull(normed_total)
@@ -329,7 +431,7 @@
     grads = []
     for which in (1, 2):
         block = jnp.stack(
-            [jnp.where(r[which], r[0], jnp.zeros_like(r[0])) for r in right], axis=1
+            [jnp.where(r[which], r[0], jnp.zeros_like(r[0])) for r in right], axis=2
         ).reshape(left.shape[0], -1)
         grads.append(
             lax.dot_general(

time: 329 us -> 259 us (0.79)
  Pallas kernels: 253 us -> 188 us
    pallas_call x1, Pallas kernels: 126 us -> 80.9 us  [front(): pl.pallas_call(functools.partial(front_kernel, n, sections), out_shape=(j...]
    pallas_call x3, Pallas kernels: 120 us -> 98.8 us  [back(): pl.pallas_call(functools.partial(back_kernel, n, sections, tick), out_sha...]
  transfers between devices with their start and end apart: 2 -> 2, of which waited for: 1 -> 1; matrix products, arithmetic and copies ran while one was open for 5% -> 8% of each run, Pallas kernels for 0% -> 0%
where the time goes in v2:
time: 259 us; the launch traced here: 258 us
  Pallas kernels  188 us (73%)
  other arithmetic  39.6 us (15%)
  matrix products  16.8 us (6%)
  local copies, waits for them, and re-layouts  10.3 us (4%)
    pallas_call x3, Pallas kernels, back(): pl.pallas_call(functools.partial(back_kernel, n, sections, tick), out_sha...  98.8 us
    pallas_call x1, Pallas kernels, front(): pl.pallas_call(functools.partial(front_kernel, n, sections), out_shape=(j...  80.9 us
    pallas_call x1, Pallas kernels, gain_sums(): pl.pallas_call(functools.partial(gain_kernel, n), out_shape=jax.ShapeDtyp...  7.9 us
    dot_general x9, matrix products, attend(): jnp.einsum('pkgd,qkd->kgpq', query_rows, key_rows, preferred_element_type...  7.22 us
    unnamed x54, local copies, waits for them, and re-layouts  6.1 us
    another operation x7, other arithmetic  5.86 us
    another operation x3, other arithmetic, body(): jnp.stack([jnp.where(r[which], r[0], jnp.zeros_like(r[0])) for r in right...  5.62 us
  transfers between devices with their start and end apart: 2, of which 1 were waited for; matrix products, arithmetic and copies ran while one was open for 8% of the time, Pallas kernels for 0%

profile of v2, /device:TPU:0, one launch (start us, length us, event | category | flops | bytes accessed | tf_op | source)
XLA Modules:
  0.0 258.0 jit_solution(5199444954333607033)
XLA Ops:
  0.7 1.2 fusion.45
  1.9 3.1 %convert_bitcast_fusion.3 = (f32[8,8,32,128]{3,1,2,0:T(8,128)}, f32[8,8,32,128]{3,1,2,0:T(8,128)S(1)}, f32[8,8,32,128]{3,1,2,0:T(8,128)}) fusion(bf16[1,1,3,64,4096]{4,3,2,1,0:T(8,128)(2,1)} %param.12), kind=kLoop, calls=%fused_computation.25 | loop fusion | flops 786432 | bytes 4718592
  5.0 0.7 constant_dynamic-slice_fusion.1
  7.4 80.9 %shard_map.85 = (f32[3,64,1024]{2,1,0:T(8,128)}, bf16[2,4,3,64,512]{4,3,2,1,0:T(8,128)(2,1)}, f32[8,2,512]{2,1,0:T(2,128)}, bf16[2,1024,1024]{2,1,0:T(8,128)(2,1)}) custom-call(bf16[3,64,4096]{2,1,0:T(8,128)(2,1)} %bitcast.445, bf16[2,512,1024]{2,1,0:T(8,128)(2,1)} %bitcast.460, f32[2,512]{1,0:T(2,128)} %bitcast_convert_fusion.g), custom_call_target="tpu_custom_call" | custom-call | tf_op jit(solution)/shard_map/pallas_call | solution.py:200
  88.2 1.1 fusion.125
  89.4 0.9 constant_dynamic-slice_fusion
  90.3 1.0 fusion.108
  91.9 0.9 fusion.40
  92.8 1.0 fusion.66
  95.0 0.8 fusion.39
  96.6 0.8 select_convert_fusion.2.kc
  97.4 32.1 %shard_map.86 = (bf16[2,4,64,1024]{3,2,1,0:T(8,128)(2,1)}, bf16[64,4096]{1,0:T(8,128)(2,1)}) custom-call(bf16[64,1024]{1,0:T(8,128)(2,1)} %select_convert_fusion.2.kc, bf16[2,1024,1024]{2,1,0:T(8,128)(2,1)} %get-tuple-element.51.w2), custom_call_target="tpu_custom_call" | custom-call | tf_op jit(solution)/shard_map/pallas_call | solution.py:293
  129.5 2.3 fusion.48
  131.8 1.8 fusion.111
  133.7 0.8 iota_compare_fusion.5
  134.5 0.7 fusion.163
  135.2 0.7 iota_compare_fusion.4
  135.8 0.7 fusion.164
  136.7 2.5 copy.86
  139.2 1.0 fusion.124
  140.4 1.2 copy.89
  141.6 2.2 fusion.109
  144.0 0.8 and_reduce_fusion
  145.6 2.7 %select_bitcast_fusion.5 = (bf16[2,4,1,64,1024]{4,3,1,0,2:T(8,128)(2,1)}, bf16[2,4,1,64,1024]{4,3,1,0,2:T(8,128)(2,1)}) fusion(bf16[2,4,64,1024]{3,2,1,0:T(8,128)(2,1)} %get-tuple-element.56, pred[]{:T(512)S(6)} %and.159, pred[]{:T(512)S(6)} %and.162), kind=kLoop, calls=%fused_computation.153 | loop fusion | flops 1048576 | bytes 3145730 | tf_op jit(solution)/shard_map/stack | solution.py:433
  149.1 0.7 fusion.76
  151.1 0.8 fusion.37
  152.2 0.7 select_convert_fusion.1.kc
  153.0 33.7 %shard_map.87 = (bf16[2,4,64,1024]{3,2,1,0:T(8,128)(2,1)}, bf16[64,4096]{1,0:T(8,128)(2,1)}) custom-call(bf16[64,1024]{1,0:T(8,128)(2,1)} %select_convert_fusion.1.kc, bf16[2,1024,1024]{2,1,0:T(8,128)(2,1)} %get-tuple-element.51.w2), custom_call_target="tpu_custom_call" | custom-call | tf_op jit(solution)/shard_map/pallas_call | solution.py:293
  187.7 1.0 fusion.52
  188.8 1.9 fusion.113
  190.6 1.0 fusion.123
  192.8 1.0 fusion.110
  194.1 1.6 select_bitcast_fusion.4
  195.7 2.0 collective-permute-done.1
  198.5 0.7 fusion.86
  199.2 0.7 fusion.101
  200.4 0.8 fusion.35
  201.6 0.7 select_convert_fusion.kc
  202.3 32.9 %shard_map.88 = (bf16[2,4,64,1024]{3,2,1,0:T(8,128)(2,1)}, bf16[64,4096]{1,0:T(8,128)(2,1)}) custom-call(bf16[64,1024]{1,0:T(8,128)(2,1)} %select_convert_fusion.kc, bf16[2,1024,1024]{2,1,0:T(8,128)(2,1)} %get-tuple-element.51.w2), custom_call_target="tpu_custom_call" | custom-call | tf_op jit(solution)/shard_map/pallas_call | solution.py:293
  236.3 0.9 fusion.56
  237.2 0.7 broadcast_select_fusion
  238.7 7.9 %shard_map.89 = f32[2,512]{1,0:T(2,128)} custom-call(f32[8,2,512]{2,1,0:T(2,128)} %bitcast.484), custom_call_target="tpu_custom_call" | custom-call | tf_op jit(solution)/shard_map/pallas_call | solution.py:334
  246.6 1.3 convert_bitcast_fusion.10
  247.9 1.4 select_bitcast_fusion.3
  249.3 3.4 %fusion.8 = f32[1,1,512,1024]{3,2,1,0:T(8,128)S(1)} fusion(bf16[2,4,3,64,512]{4,3,2,1,0:T(8,128)(2,1)} %get-tuple-element.55, bf16[2,4,1,64,1024]{4,3,1,0,2:T(8,128)(2,1)S(1)} %get-tuple-element.84, bf16[2,4,1,64,1024]{4,3,1,0,2:T(8,128)(2,1)S(1)} %copy-done.15, bf16[2,4,1,64,1024]{4,3,1,0,2:T(8,128)(2,1)S(1)} %copy-done.13), kind=kOutput, calls=%fused_computation.9 | convolution fusion | flops 1613758464 | bytes 6815744 | tf_op jit(solution)/shard_map/dot_general | solution.py:437
  252.7 1.8 fusion.5
  254.5 1.6 fusion
  256.1 1.8 fusion.114
  (123 shorter events, 13.8 us)
Async XLA Ops:
  1.9 3.1 %copy-start.21 = (s32[4,1,64]{2,1,0:T(1,128)S(1)}, s32[4,1,64]{2,1,0:T(1,128)}, u32[]{:S(2)}) copy-start(s32[4,1,64]{2,1,0:T(1,128)} %param.17) | copy-start | bytes 3076
  1.9 3.1 %copy-start.19 = (s32[4,1]{0,1:T(1,128)S(1)}, s32[4,1]{0,1:T(1,128)}, u32[]{:S(2)}) copy-start(s32[4,1]{0,1:T(1,128)} %param.16) | copy-start | bytes 52
  5.0 1.8 copy-start.20
  88.2 3.4 %copy-start.4 = (bf16[1,1,64,4096]{3,2,1,0:T(8,128)(2,1)S(1)}, bf16[1,1,64,4096]{3,2,1,0:T(8,128)(2,1)}, u32[]{:S(2)}) copy-start(bf16[1,1,64,4096]{3,2,1,0:T(8,128)(2,1)} %param.13) | copy-start | bytes 1572868
  97.3 32.2 %copy-start = (bf16[1,1,3,64,4096]{4,3,2,1,0:T(8,128)(2,1)S(1)}, bf16[1,1,3,64,4096]{4,3,2,1,0:T(8,128)(2,1)}, u32[]{:S(2)}) copy-start(bf16[1,1,3,64,4096]{4,3,2,1,0:T(8,128)(2,1)} %param.12) | copy-start | bytes 4718596
  129.5 2.3 copy-start.11
  133.7 6.7 %copy-start.3 = (f32[8,8,32,128]{3,1,2,0:T(8,128)S(1)}, f32[8,8,32,128]{3,1,2,0:T(8,128)}, u32[]{:S(2)}) copy-start(f32[8,8,32,128]{3,1,2,0:T(8,128)} %get-tuple-element.76) | copy-start | bytes 3145732
  133.7 14.6 %collective-permute-start = (bf16[64,4096]{1,0:T(8,128)(2,1)}, bf16[64,4096]{1,0:T(8,128)(2,1)S(1)}, u32[]{:S(2)}, u32[]{:S(2)}) collective-permute-start(bf16[64,4096]{1,0:T(8,128)(2,1)} %fusion.111), channel_id=1, source_target_pairs={{0,24},{8,0},{16,8},{24,16},{1,25},{9,1},{17,9},{25,17},{2,26},{10... | collective-permute-start | bytes 1572872 | tf_op jit(solution)/shard_map/ppermute | solution.py:20
  141.6 2.5 copy-start.22
  148.3 0.8 copy-start.5
  149.9 1.2 copy-start.2
  186.7 1.0 copy-start.10
  187.0 1.8 copy-start.6
  188.8 4.1 %copy-start.1 = (f32[8,8,32,128]{3,2,1,0:T(8,128)S(1)}, f32[8,8,32,128]{3,2,1,0:T(8,128)}, u32[]{:S(2)}) copy-start(f32[8,8,32,128]{3,2,1,0:T(8,128)} %copy.89) | copy-start | bytes 3145732
  190.6 7.0 %collective-permute-start.1 = (bf16[64,4096]{1,0:T(8,128)(2,1)}, bf16[64,4096]{1,0:T(8,128)(2,1)S(1)}, u32[]{:S(2)}, u32[]{:S(2)}) collective-permute-start(bf16[64,4096]{1,0:T(8,128)(2,1)} %fusion.113), channel_id=1, source_target_pairs={{0,24},{8,0},{16,8},{24,16},{1,25},{9,1},{17,9},{25,17},{2,26},{10... | collective-permute-start | bytes 1572872 | tf_op jit(solution)/shard_map/ppermute | solution.py:20
  192.8 1.3 copy-start.16
  197.7 0.8 copy-start.7
  235.3 1.0 copy-start.9
  238.1 0.6 copy-start.17
  238.1 11.1 %copy-start.13 = (bf16[2,4,1,64,1024]{4,3,1,0,2:T(8,128)(2,1)S(1)}, bf16[2,4,1,64,1024]{4,3,1,0,2:T(8,128)(2,1)}, u32[]{:S(2)}) copy-start(bf16[2,4,1,64,1024]{4,3,1,0,2:T(8,128)(2,1)} %get-tuple-element.80) | copy-start | bytes 3145732
  238.1 11.1 %copy-start.15 = (bf16[2,4,1,64,1024]{4,3,1,0,2:T(8,128)(2,1)S(1)}, bf16[2,4,1,64,1024]{4,3,1,0,2:T(8,128)(2,1)}, u32[]{:S(2)}) copy-start(bf16[2,4,1,64,1024]{4,3,1,0,2:T(8,128)(2,1)} %get-tuple-element.82) | copy-start | bytes 3145732
  249.2 3.4 %copy-start.12 = (bf16[2,4,1,64,1024]{4,3,1,0,2:T(8,128)(2,1)S(1)}, bf16[2,4,1,64,1024]{4,3,1,0,2:T(8,128)(2,1)}, u32[]{:S(2)}) copy-start(bf16[2,4,1,64,1024]{4,3,1,0,2:T(8,128)(2,1)} %get-tuple-element.79) | copy-start | bytes 3145732
  249.2 3.4 %copy-start.14 = (bf16[2,4,1,64,1024]{4,3,1,0,2:T(8,128)(2,1)S(1)}, bf16[2,4,1,64,1024]{4,3,1,0,2:T(8,128)(2,1)}, u32[]{:S(2)}) copy-start(bf16[2,4,1,64,1024]{4,3,1,0,2:T(8,128)(2,1)} %get-tuple-element.81) | copy-start | bytes 3145732
  249.3 3.4 %copy-start.23 = (bf16[2,4,3,64,512]{4,3,2,1,0:T(8,128)(2,1)S(1)}, bf16[2,4,3,64,512]{4,3,2,1,0:T(8,128)(2,1)}, u32[]{:S(2)}) copy-start(bf16[2,4,3,64,512]{4,3,2,1,0:T(8,128)(2,1)} %get-tuple-element.55) | copy-start | bytes 4718596
  252.7 1.8 copy-start.18
  254.5 1.6 copy-start.8

commit v3 on v2

--- a/solution.py
+++ b/solution.py
@@ -306,8 +306,11 @@
     )(kc, w2)
 
 
-def gain_kernel(n, sums, out, got, ss, sr):
+def tail_kernel(
+    n, sections, sums, cols, first, second, third, g, grad, gain, got, acc, ss, sr
+):
     me = lax.axis_index("fsdp")
+    section = lax.axis_index("pipe")
     greet_all(n, me)
 
     def copy(k):
@@ -319,29 +322,45 @@
         return 0
 
     lax.fori_loop(1, n, send, 0)
-    out[...] = sums[me]
+    acc[...] = jnp.zeros_like(acc)
+    for tick, rows in enumerate((first, second, third)):
+        stretch = stretch_of(section, tick, sections)
+        left = cols[:, :, tick].reshape(-1, cols.shape[-1])
+        right = rows[...].reshape(left.shape[0], -1)
+        acc[stretch] += lax.dot_general(
+            left, right, (((0,), (0,)), ((), ())), preferred_element_type=jnp.float32
+        )
+    grad[...] = (acc[...] * g[...]).astype(jnp.bfloat16)
+    gain[...] = sums[me]
 
     def collect(k, _):
         copy(k).wait()
-        out[...] += got[k]
+        gain[...] += got[k]
         return 0
 
     lax.fori_loop(1, n, collect, 0)
 
 
-def gain_sums(n, sums):
+def tail(n, sections, sums, cols, rows, g):
+    kvw = rows[0].shape[-1]
     vmem = pl.BlockSpec(memory_space=pltpu.VMEM)
     return pl.pallas_call(
-        functools.partial(gain_kernel, n),
-        out_shape=jax.ShapeDtypeStruct(sums.shape[1:], jnp.float32),
-        in_specs=[vmem],
-        out_specs=vmem,
-        scratch_shapes=[pltpu.VMEM(sums.shape, jnp.float32)]
+        functools.partial(tail_kernel, n, sections),
+        out_shape=(
+            jax.ShapeDtypeStruct((2, cols.shape[-1], kvw), jnp.bfloat16),
+            jax.ShapeDtypeStruct(sums.shape[1:], jnp.float32),
+        ),
+        in_specs=[vmem] * 6,
+        out_specs=(vmem,) * 2,
+        scratch_shapes=[
+            pltpu.VMEM(sums.shape, jnp.float32),
+            pltpu.VMEM((2, cols.shape[-1], kvw), jnp.float32),
+        ]
         + [pltpu.SemaphoreType.DMA((n,))] * 2,
         compiler_params=pltpu.CompilerParams(
             collective_id=1 + TICKS, has_side_effects=True, vmem_limit_bytes=LIMIT
         ),
-    )(sums)
+    )(sums, cols, *rows, g)
 
 
 def normalize(resid, gain):
@@ -417,7 +436,7 @@
         direct, normed_cot, keyval_cot = pull(carried.astype(jnp.float32))
         scaled = jnp.where(active, keyval_cot * factor, 0.0).astype(jnp.bfloat16)
         rows_all, product = back(n, sections, tick, scaled, w2)
-        right.append((rows_all, active & (stretch == 0), active & (stretch == 1)))
+        right.append(rows_all)
         normed_total = normed_cot + product.astype(jnp.float32) / factor
         resid_cot, gain_cot = front_pull(normed_total)
         acc_gain = acc_gain.at[stretch].add(jnp.where(active, gain_cot, 0.0))
@@ -426,19 +445,9 @@
             carried = passed_along(carried, "pipe", -1)
     width = w.shape[1]
     sums = jnp.swapaxes(acc_gain.reshape(2, n, width), 0, 1)
-    grad_gain = gain_sums(n, sums).astype(jnp.bfloat16)[:, None]
-    left = cols.reshape(-1, width)
-    grads = []
-    for which in (1, 2):
-        block = jnp.stack(
-            [jnp.where(r[which], r[0], jnp.zeros_like(r[0])) for r in right], axis=2
-        ).reshape(left.shape[0], -1)
-        grads.append(
-            lax.dot_general(
-                left, block, (((0,), (0,)), ((), ())), preferred_element_type=jnp.float32
-            )
-        )
-    grad_kv = (jnp.stack(grads) * own_gain[:, :, None]).astype(jnp.bfloat16)[:, None]
+    grad_kv, grad_gain = tail(n, sections, sums, cols, right, own_gain[:, :, None])
+    grad_kv = grad_kv[:, None]
+    grad_gain = grad_gain.astype(jnp.bfloat16)[:, None]
     return (carried[None, None], grad_kv, grad_gain)
 
 

time: 259 us -> 252 us (0.973)
  other arithmetic: 39.6 us -> 31.8 us
  matrix products: 16.8 us -> 12.8 us
    another operation x10 -> x7, other arithmetic: 11.5 us -> 5.74 us
    dot_general x2 -> x0, matrix products: 5.17 us -> none  [body(): lax.dot_general(left, block, (((0,), (0,)), ((), ())), preferred_element_...]
    unnamed x54 -> x43, local copies, waits for them, and re-layouts: 6.1 us -> 7.53 us
  transfers between devices with their start and end apart: 2 -> 2, of which waited for: 1 -> 1; matrix products, arithmetic and copies ran while one was open for 8% -> 7% of each run, Pallas kernels for 0% -> 0%
where the time goes in v3:
time: 252 us
  Pallas kernels  190 us (75%)
  other arithmetic  31.8 us (13%)
  matrix products  12.8 us (5%)
  local copies, waits for them, and re-layouts  12.7 us (5%)
    pallas_call x3, Pallas kernels, back(): pl.pallas_call(functools.partial(back_kernel, n, sections, tick), out_sha...  98.9 us
    pallas_call x1, Pallas kernels, front(): pl.pallas_call(functools.partial(front_kernel, n, sections), out_shape=(j...  80.9 us
    pallas_call x1, Pallas kernels, tail(): pl.pallas_call(functools.partial(tail_kernel, n, sections), out_shape=(ja...  10.4 us
    dot_general x9, matrix products, attend(): jnp.einsum('pkgd,qkd->kgpq', query_rows, key_rows, preferred_element_type...  8.43 us
    unnamed x43, local copies, waits for them, and re-layouts  7.53 us
    another operation x7, other arithmetic  5.74 us
  transfers between devices with their start and end apart: 2, of which 1 were waited for; matrix products, arithmetic and copies ran while one was open for 7% of the time, Pallas kernels for 0%

profile of v3, /device:TPU:0, one launch (start us, length us, event | category | flops | bytes accessed | tf_op | source)
XLA Modules:
  0.0 251.6 jit_solution(14290318361324486349)
XLA Ops:
  0.7 1.2 fusion.34
  1.9 3.0 %convert_bitcast_fusion.3 = (f32[8,8,32,128]{3,1,2,0:T(8,128)}, f32[8,8,32,128]{3,1,2,0:T(8,128)S(1)}, f32[8,8,32,128]{3,1,2,0:T(8,128)}) fusion(bf16[1,1,3,64,4096]{4,3,2,1,0:T(8,128)(2,1)} %param.12), kind=kLoop, calls=%fused_computation.15 | loop fusion | flops 786432 | bytes 4718592
  5.0 0.6 constant_dynamic-slice_fusion.1
  5.6 0.6 iota_compare_fusion.6
  7.3 80.9 %shard_map.85 = (f32[3,64,1024]{2,1,0:T(8,128)}, bf16[2,4,3,64,512]{4,3,2,1,0:T(8,128)(2,1)}, f32[8,2,512]{2,1,0:T(2,128)}, bf16[2,1024,1024]{2,1,0:T(8,128)(2,1)}) custom-call(bf16[3,64,4096]{2,1,0:T(8,128)(2,1)} %bitcast.423, bf16[2,512,1024]{2,1,0:T(8,128)(2,1)} %bitcast.438, f32[2,512]{1,0:T(2,128)} %get-tuple-element.105.g), custom_call_target="tpu_custom_call" | custom-call | tf_op jit(solution)/shard_map/pallas_call | solution.py:200
  88.2 1.0 fusion.114
  89.3 0.9 constant_dynamic-slice_fusion
  90.3 1.0 fusion.97
  91.8 0.9 fusion.29
  92.7 1.0 fusion.55
  93.8 0.6 fusion.92
  95.0 0.8 fusion.28
  96.5 0.8 select_convert_fusion.2.kc
  97.3 32.2 %shard_map.86 = (bf16[2,4,64,1024]{3,2,1,0:T(8,128)(2,1)}, bf16[64,4096]{1,0:T(8,128)(2,1)}) custom-call(bf16[64,1024]{1,0:T(8,128)(2,1)} %select_convert_fusion.2.kc, bf16[2,1024,1024]{2,1,0:T(8,128)(2,1)} %get-tuple-element.53.w2), custom_call_target="tpu_custom_call" | custom-call | tf_op jit(solution)/shard_map/pallas_call | solution.py:293
  129.5 2.3 fusion.37
  131.8 1.8 fusion.100
  133.6 0.7 iota_compare_fusion.4
  135.1 1.2 copy.115
  136.2 1.0 fusion.113
  137.3 0.8 and_reduce_fusion
  138.1 0.6 select_select_fusion
  138.7 2.2 fusion.98
  141.6 2.5 copy.118
  144.1 1.0 copy.70.g
  145.3 0.7 fusion.153
  147.1 0.7 fusion.65
  147.8 0.6 fusion.91
  149.1 0.8 fusion.26
  150.2 0.7 select_convert_fusion.1.kc
  151.0 33.8 %shard_map.87 = (bf16[2,4,64,1024]{3,2,1,0:T(8,128)(2,1)}, bf16[64,4096]{1,0:T(8,128)(2,1)}) custom-call(bf16[64,1024]{1,0:T(8,128)(2,1)} %select_convert_fusion.1.kc, bf16[2,1024,1024]{2,1,0:T(8,128)(2,1)} %get-tuple-element.53.w2), custom_call_target="tpu_custom_call" | custom-call | tf_op jit(solution)/shard_map/pallas_call | solution.py:293
  185.2 0.6 copy-done.11
  185.8 1.0 fusion.41
  186.8 1.9 fusion.102
  188.7 1.0 fusion.112
  190.4 2.2 fusion.99
  193.3 2.4 collective-permute-done.1
  196.5 0.7 fusion.75
  197.3 0.6 fusion.90
  198.5 0.8 fusion.24
  199.6 0.7 select_convert_fusion.kc
  200.4 33.0 %shard_map.88 = (bf16[2,4,64,1024]{3,2,1,0:T(8,128)(2,1)}, bf16[64,4096]{1,0:T(8,128)(2,1)}) custom-call(bf16[64,1024]{1,0:T(8,128)(2,1)} %select_convert_fusion.kc, bf16[2,1024,1024]{2,1,0:T(8,128)(2,1)} %get-tuple-element.53.w2), custom_call_target="tpu_custom_call" | custom-call | tf_op jit(solution)/shard_map/pallas_call | solution.py:293
  233.8 0.6 copy-done.10
  234.4 0.9 fusion.45
  235.3 0.7 broadcast_select_fusion
  236.8 10.4 %shard_map.89 = (bf16[2,512,1024]{2,1,0:T(8,128)(2,1)}, f32[2,512]{1,0:T(2,128)}) custom-call(f32[8,2,512]{2,1,0:T(2,128)} %bitcast.463, bf16[2,4,3,64,512]{4,3,2,1,0:T(8,128)(2,1)} %get-tuple-element.57.cols, bf16[2,4,64,1024]{3,2,1,0:T(8,128)(2,1)} %get-tuple-element.58.first, bf16[2,4,64,1024]{3,2,1,0:T(8,128)(2,1)} %get-tuple-element.59.second, ...), custom_call_target="tpu_custom_call" | custom-call | tf_op jit(solution)/shard_map/pallas_call | solution.py:347
  247.2 1.3 convert_bitcast_fusion.12
  248.4 1.8 fusion.103
  250.3 1.3 copy.243
  (107 shorter events, 11.2 us)
Async XLA Ops:
  1.9 3.1 %copy-start.16 = (s32[4,1,64]{2,1,0:T(1,128)S(1)}, s32[4,1,64]{2,1,0:T(1,128)}, u32[]{:S(2)}) copy-start(s32[4,1,64]{2,1,0:T(1,128)} %param.17) | copy-start | bytes 3076
  1.9 3.1 %copy-start.14 = (s32[4,1]{0,1:T(1,128)S(1)}, s32[4,1]{0,1:T(1,128)}, u32[]{:S(2)}) copy-start(s32[4,1]{0,1:T(1,128)} %param.16) | copy-start | bytes 52
  5.0 1.7 copy-start.15
  90.2 1.3 copy-start.4
  97.3 32.2 %copy-start = (bf16[1,1,3,64,4096]{4,3,2,1,0:T(8,128)(2,1)S(1)}, bf16[1,1,3,64,4096]{4,3,2,1,0:T(8,128)(2,1)}, u32[]{:S(2)}) copy-start(bf16[1,1,3,64,4096]{4,3,2,1,0:T(8,128)(2,1)} %param.12) | copy-start | bytes 4718596
  129.4 2.3 copy-start.12
  131.8 3.3 %copy-start.3 = (f32[8,8,32,128]{3,1,2,0:T(8,128)S(1)}, f32[8,8,32,128]{3,1,2,0:T(8,128)}, u32[]{:S(2)}) copy-start(f32[8,8,32,128]{3,1,2,0:T(8,128)} %get-tuple-element.88) | copy-start | bytes 3145732
  133.6 3.7 %copy-start.17 = (s32[2]{0:T(128)S(1)}, s32[2]{0:T(128)}, u32[]{:S(2)}) copy-start(s32[2]{0:T(128)} %constant.172.clone.1) | copy-start | bytes 28
  133.6 12.6 %collective-permute-start = (bf16[64,4096]{1,0:T(8,128)(2,1)}, bf16[64,4096]{1,0:T(8,128)(2,1)S(1)}, u32[]{:S(2)}, u32[]{:S(2)}) collective-permute-start(bf16[64,4096]{1,0:T(8,128)(2,1)} %fusion.100), channel_id=1, source_target_pairs={{0,24},{8,0},{16,8},{24,16},{1,25},{9,1},{17,9},{25,17},{2,26},{10... | collective-permute-start | bytes 1572872 | tf_op jit(solution)/shard_map/ppermute | solution.py:20
  146.3 0.8 copy-start.5
  147.8 1.2 copy-start.2
  184.8 1.0 copy-start.11
  185.2 1.6 copy-start.6
  188.7 7.0 %collective-permute-start.1 = (bf16[64,4096]{1,0:T(8,128)(2,1)}, bf16[64,4096]{1,0:T(8,128)(2,1)S(1)}, u32[]{:S(2)}, u32[]{:S(2)}) collective-permute-start(bf16[64,4096]{1,0:T(8,128)(2,1)} %fusion.102), channel_id=1, source_target_pairs={{0,24},{8,0},{16,8},{24,16},{1,25},{9,1},{17,9},{25,17},{2,26},{10... | collective-permute-start | bytes 1572872 | tf_op jit(solution)/shard_map/ppermute | solution.py:20
  195.7 0.8 copy-start.7
  197.3 1.2 copy-start.1
  233.4 1.0 copy-start.10
  236.2 0.6 copy-start.13
  236.8 11.7 %copy-start.8 = (bf16[64,4096]{1,0:T(8,128)(2,1)S(1)}, bf16[64,4096]{1,0:T(8,128)(2,1)}, u32[]{:S(2)}) copy-start(bf16[64,4096]{1,0:T(8,128)(2,1)} %copy-done.7) | copy-start | bytes 1572868
  248.4 1.8 copy-start.9

commit v4 on v3

--- a/solution.py
+++ b/solution.py
@@ -368,42 +368,75 @@
     return resid * factor * gain
 
 
-def attend(resid, normalized_input, key_value_pair, length, segment):
-    item_count = resid.shape[0]
-    model_width = resid.shape[1]
-    query_groups = model_width // HEAD_SIZE // KEY_VALUE_HEADS
-    query_rows = normalized_input.astype(jnp.bfloat16).reshape(
-        item_count, KEY_VALUE_HEADS, query_groups, HEAD_SIZE
-    )
-    key_rows = (
-        key_value_pair[:, : KEY_VALUE_HEADS * HEAD_SIZE]
-        .astype(jnp.bfloat16)
-        .reshape(item_count, KEY_VALUE_HEADS, HEAD_SIZE)
-    )
-    value_rows = (
-        key_value_pair[:, KEY_VALUE_HEADS * HEAD_SIZE :]
-        .astype(jnp.bfloat16)
-        .reshape(item_count, KEY_VALUE_HEADS, HEAD_SIZE)
-    )
-    scores = jnp.einsum(
-        "pkgd,qkd->kgpq", query_rows, key_rows, preferred_element_type=jnp.float32
-    ) * HEAD_SIZE ** (-0.5)
-    place = jnp.arange(item_count, dtype=jnp.int32)
-    allowed = (
-        (segment[:, None] == segment[None, :])
-        & (place[None, :] <= place[:, None])
-        & (place[None, :] < length)
-    )
-    allowed = allowed | (place[:, None] == place[None, :])
-    scores = jnp.where(allowed, scores, -1e30)
-    peak = jnp.max(scores, axis=-1, keepdims=True)
-    expo = jnp.exp(scores - peak)
-    probs = (expo / jnp.sum(expo, axis=-1, keepdims=True)).astype(jnp.bfloat16)
-    mixed = jnp.einsum(
-        "kgpq,qkd->pkgd", probs, value_rows, preferred_element_type=jnp.float32
-    ).reshape(item_count, model_width)
-    valid = (place < length).astype(jnp.float32)
-    return resid + mixed * valid[:, None]
+def attend_kernel(x, gain, raw, cot, allowed, valid, kc, ncot):
+    rows, model = x.shape
+    groups = model // HEAD_SIZE // KEY_VALUE_HEADS
+    half = KEY_VALUE_HEADS * HEAD_SIZE
+    resid = x[...].astype(jnp.float32)
+    factor = lax.rsqrt(jnp.mean(resid * resid, axis=-1, keepdims=True) + EPS)
+    normed = (resid * factor * gain[...]).astype(jnp.bfloat16)
+    mixed_cot = (cot[...].astype(jnp.float32) * valid[...]).astype(jnp.bfloat16)
+    seen = jnp.concatenate([allowed[...]] * groups, axis=0) > 0.5
+    across = (((1,), (1,)), ((), ()))
+    down = (((0,), (0,)), ((), ()))
+
+    def heads(value, at):
+        first = at * groups
+        return jnp.concatenate(
+            [
+                value[:, (first + i) * HEAD_SIZE : (first + i + 1) * HEAD_SIZE]
+                for i in range(groups)
+            ],
+            axis=0,
+        )
+
+    for at in range(KEY_VALUE_HEADS):
+        key_at = slice(at * HEAD_SIZE, (at + 1) * HEAD_SIZE)
+        value_at = slice(half + at * HEAD_SIZE, half + (at + 1) * HEAD_SIZE)
+        keys = (raw[:, key_at] * factor).astype(jnp.bfloat16)
+        values = (raw[:, value_at] * factor).astype(jnp.bfloat16)
+        query = heads(normed, at)
+        pulled = heads(mixed_cot, at)
+        scores = lax.dot_general(query, keys, across, preferred_element_type=jnp.float32)
+        scores = jnp.where(seen, scores * HEAD_SIZE ** (-0.5), -1e30)
+        expo = jnp.exp(scores - jnp.max(scores, axis=-1, keepdims=True))
+        probs = expo / jnp.sum(expo, axis=-1, keepdims=True)
+        prob_cot = lax.dot_general(
+            pulled, values, across, preferred_element_type=jnp.float32
+        )
+        prob_cot = prob_cot.astype(jnp.bfloat16).astype(jnp.float32)
+        inner = jnp.sum(probs * prob_cot, axis=-1, keepdims=True)
+        score_cot = jnp.where(seen, probs * (prob_cot - inner), 0.0) * HEAD_SIZE ** (-0.5)
+        score_cot = score_cot.astype(jnp.bfloat16)
+        query_cot = jnp.dot(score_cot, keys, preferred_element_type=jnp.float32)
+        for i in range(groups):
+            head = at * groups + i
+            ncot[:, head * HEAD_SIZE : (head + 1) * HEAD_SIZE] = query_cot[
+                i * rows : (i + 1) * rows
+            ].astype(jnp.bfloat16)
+        key_cot = lax.dot_general(score_cot, query, down, preferred_element_type=jnp.float32)
+        value_cot = lax.dot_general(
+            probs.astype(jnp.bfloat16), pulled, down, preferred_element_type=jnp.float32
+        )
+        kc[:, key_at] = (key_cot * factor).astype(jnp.bfloat16)
+        kc[:, value_at] = (value_cot * factor).astype(jnp.bfloat16)
+
+
+def attend_back(x, gain, raw, cot, allowed, valid):
+    vmem = pl.BlockSpec(memory_space=pltpu.VMEM)
+    return pl.pallas_call(
+        attend_kernel,
+        out_shape=(
+            jax.ShapeDtypeStruct(raw.shape, jnp.bfloat16),
+            jax.ShapeDtypeStruct(x.shape, jnp.bfloat16),
+        ),
+        in_specs=[vmem] * 6,
+        out_specs=(vmem,) * 2,
+        cost_estimate=pl.CostEstimate(
+            flops=500_000_000, bytes_accessed=3_000_000, transcendentals=200_000
+        ),
+        compiler_params=pltpu.CompilerParams(vmem_limit_bytes=LIMIT),
+    )(x, gain, raw, cot, allowed, valid)
 
 
 def body(saved, cot_in, weights, gains, lengths, segments):
@@ -427,20 +460,24 @@
         segment = segments[item, 0]
         resid = saved[0, 0, tick].astype(jnp.float32)
         factor = lax.rsqrt(jnp.mean(resid * resid, axis=-1, keepdims=True) + EPS)
-        normalized_input, front_pull = jax.vjp(normalize, resid, whole_g[stretch])
-
-        def inner(first, second, third):
-            return attend(first, second, third, length, segment)
-
-        _, pull = jax.vjp(inner, resid, normalized_input, kv[tick] * factor)
-        direct, normed_cot, keyval_cot = pull(carried.astype(jnp.float32))
-        scaled = jnp.where(active, keyval_cot * factor, 0.0).astype(jnp.bfloat16)
+        _, front_pull = jax.vjp(normalize, resid, whole_g[stretch])
+        place = jnp.arange(resid.shape[0], dtype=jnp.int32)
+        allowed = (
+            (segment[:, None] == segment[None, :])
+            & (place[None, :] <= place[:, None])
+            & (place[None, :] < length)
+        )
+        allowed = (allowed | (place[:, None] == place[None, :])).astype(jnp.float32)
+        valid = ((place < length) & active).astype(jnp.float32)[:, None]
+        scaled, normed_cot = attend_back(
+            saved[0, 0, tick], whole_g[stretch][None], kv[tick], carried, allowed, valid
+        )
         rows_all, product = back(n, sections, tick, scaled, w2)
         right.append(rows_all)
-        normed_total = normed_cot + product.astype(jnp.float32) / factor
+        normed_total = normed_cot.astype(jnp.float32) + product.astype(jnp.float32) / factor
         resid_cot, gain_cot = front_pull(normed_total)
         acc_gain = acc_gain.at[stretch].add(jnp.where(active, gain_cot, 0.0))
-        carried = jnp.where(active, (direct + resid_cot).astype(jnp.bfloat16), carried)
+        carried = jnp.where(active, (carried.astype(jnp.float32) + resid_cot).astype(jnp.bfloat16), carried)
         if tick + 1 < TICKS:
             carried = passed_along(carried, "pipe", -1)
     width = w.shape[1]

time: 252 us -> 244 us (0.968)
  Pallas kernels: 190 us -> 203 us
  matrix products: 12.8 us -> 0 us
  other arithmetic: 31.8 us -> 21.4 us
  waiting for transfers between devices: 2.43 us -> 5.83 us
    pallas_call x0 -> x3, Pallas kernels: none -> 13.2 us  [attend_back(): pl.pallas_call(attend_kernel, out_shape=(jax.ShapeDtypeStruct(raw.shape,...]
    dot_general x15 -> x0, matrix products: 12.8 us -> none  [the longest x9 8.43 us: attend(): jnp.einsum('pkgd,qkd->kgpq', query_rows, key_rows, preferred_element_type...]
    squeeze x0 -> x2, local copies, waits for them, and re-layouts: none -> 4.63 us  [the longest x1 2.56 us: body(): saved[0, 0, tick]]
    unnamed x43 -> x45, local copies, waits for them, and re-layouts: 7.53 us -> 3.6 us
    unnamed x4 -> x0, other arithmetic: 3.47 us -> none
    ppermute x2, waiting for transfers between devices: 2.43 us -> 5.83 us  [passed_along(): lax.ppermute(value, axis, [(i, (i + by) % size) for i in range(size)])]
    another operation x7 -> x4, other arithmetic: 5.74 us -> 2.74 us
    reduce_sum x6 -> x0, other arithmetic: 2.62 us -> none  [the longest x3 1.88 us: attend(): expo = jnp.exp(scores - peak)]
  transfers between devices with their start and end apart: 2 -> 2, of which waited for: 1 -> 1; matrix products, arithmetic and copies ran while one was open for 7% -> 4% of each run, Pallas kernels for 0% -> 0%
where the time goes in v4:
time: 244 us; the launch traced here: 243 us
  Pallas kernels  203 us (83%)
  other arithmetic  21.4 us (9%)
  local copies, waits for them, and re-layouts  11.3 us (5%)
  waiting for transfers between devices  5.83 us (2%)
    pallas_call x3, Pallas kernels, back(): pl.pallas_call(functools.partial(back_kernel, n, sections, tick), out_sha...  98.8 us
    pallas_call x1, Pallas kernels, front(): pl.pallas_call(functools.partial(front_kernel, n, sections), out_shape=(j...  80.9 us
    pallas_call x3, Pallas kernels, attend_back(): pl.pallas_call(attend_kernel, out_shape=(jax.ShapeDtypeStruct(raw.shape,...  13.2 us
    pallas_call x1, Pallas kernels, tail(): pl.pallas_call(functools.partial(tail_kernel, n, sections), out_shape=(ja...  10.5 us
    ppermute x2, waiting for transfers between devices, passed_along(): lax.ppermute(value, axis, [(i, (i + by) % size) for i in range(size)])  5.83 us
    reduce_sum x3, other arithmetic, normalize(): return resid * factor * gain  5.17 us
  transfers between devices with their start and end apart: 2, of which 1 were waited for; matrix products, arithmetic and copies ran while one was open for 4% of the time, Pallas kernels for 0%

profile of v4, /device:TPU:0, one launch (start us, length us, event | category | flops | bytes accessed | tf_op | source)
XLA Modules:
  0.0 243.1 jit_solution(5514470943894428111)
XLA Ops:
  0.8 2.6 %slice_bitcast_fusion = (bf16[64,4096]{1,0:T(8,128)(2,1)}, bf16[64,4096]{1,0:T(8,128)(2,1)}, bf16[64,4096]{1,0:T(8,128)(2,1)}) fusion(bf16[1,1,3,64,4096]{4,3,2,1,0:T(8,128)(2,1)} %param.12), kind=kLoop, calls=%fused_computation.40 | loop fusion | bytes 3145728 | tf_op jit(solution)/shard_map/squeeze | solution.py:473
  3.4 1.2 fusion.6
  4.6 0.6 convert_bitcast_fusion
  5.2 0.7 constant_dynamic-slice_fusion
  5.9 0.6 iota_compare_fusion.7
  6.5 1.3 fusion.35.valid
  7.8 80.9 %shard_map.85 = (f32[3,64,1024]{2,1,0:T(8,128)}, bf16[2,4,3,64,512]{4,3,2,1,0:T(8,128)(2,1)}, f32[8,2,512]{2,1,0:T(2,128)}, bf16[2,1024,1024]{2,1,0:T(8,128)(2,1)}) custom-call(bf16[3,64,4096]{2,1,0:T(8,128)(2,1)} %bitcast.75, bf16[2,512,1024]{2,1,0:T(8,128)(2,1)} %bitcast.76, f32[2,512]{1,0:T(2,128)} %get-tuple-element.105.g), custom_call_target="tpu_custom_call" | custom-call | tf_op jit(solution)/shard_map/pallas_call | solution.py:200
  88.7 2.1 slice_bitcast_fusion.3
  90.8 0.7 fusion.29.allowed
  91.5 0.7 constant_dynamic-slice_fusion.2
  92.1 4.4 %shard_map.86 = (bf16[64,1024]{1,0:T(8,128)(2,1)}, bf16[64,4096]{1,0:T(8,128)(2,1)}) custom-call(bf16[64,4096]{1,0:T(8,128)(2,1)} %get-tuple-element.96.x, f32[1,4096]{1,0:T(1,128)} %get-tuple-element.103.gain, f32[64,1024]{1,0:T(8,128)} %get-tuple-element.100.raw, bf16[64,4096]{1,0:T(8,128)(2,1)} %bitcast.78, f32[64,64]{1,0:T(8,128)} %fusion.29.allowed, ...), custom_call_target="tpu_custom_call" | custom-call | flops 500000000 | bytes 3000000 | tf_op jit(solution)/shard_map/pallas_call | solution.py:427
  96.5 32.2 %shard_map.87 = (bf16[2,4,64,1024]{3,2,1,0:T(8,128)(2,1)}, bf16[64,4096]{1,0:T(8,128)(2,1)}) custom-call(bf16[64,1024]{1,0:T(8,128)(2,1)} %get-tuple-element.60.kc, bf16[2,1024,1024]{2,1,0:T(8,128)(2,1)} %get-tuple-element.61.w2), custom_call_target="tpu_custom_call" | custom-call | tf_op jit(solution)/shard_map/pallas_call | solution.py:293
  128.8 0.0 copy-start.8
  128.8 1.8 fusion.9
  130.6 0.0 copy-start.21
  130.6 0.5 fusion.20
  131.2 0.1 collective-permute-start
  131.2 0.7 iota_compare_fusion.6
  131.9 1.3 fusion.37.valid
  133.3 1.1 copy.15.g
  134.3 1.2 fusion.39.valid
  135.5 0.8 and_reduce_fusion
  136.3 0.6 select_select_fusion
  137.0 0.3 scatter-add.10
  137.3 0.6 iota_compare_fusion.5
  137.9 0.7 fusion.31.allowed
  138.6 0.7 fusion.33.allowed
  139.3 0.8 copy-done.11
  140.1 4.4 %shard_map.88 = (bf16[64,1024]{1,0:T(8,128)(2,1)}, bf16[64,4096]{1,0:T(8,128)(2,1)}) custom-call(bf16[64,4096]{1,0:T(8,128)(2,1)} %get-tuple-element.97.x, f32[1,4096]{1,0:T(1,128)} %get-tuple-element.102.gain, f32[64,1024]{1,0:T(8,128)} %get-tuple-element.99.raw, bf16[64,4096]{1,0:T(8,128)(2,1)} %copy-done.11, f32[64,64]{1,0:T(8,128)} %fusion.31.allowed, ...), custom_call_target="tpu_custom_call" | custom-call | flops 500000000 | bytes 3000000 | tf_op jit(solution)/shard_map/pallas_call | solution.py:427
  144.5 33.8 %shard_map.89 = (bf16[2,4,64,1024]{3,2,1,0:T(8,128)(2,1)}, bf16[64,4096]{1,0:T(8,128)(2,1)}) custom-call(bf16[64,1024]{1,0:T(8,128)(2,1)} %get-tuple-element.64.kc, bf16[2,1024,1024]{2,1,0:T(8,128)(2,1)} %get-tuple-element.61.w2), custom_call_target="tpu_custom_call" | custom-call | tf_op jit(solution)/shard_map/pallas_call | solution.py:293
  178.4 1.8 fusion.13
  180.2 0.5 fusion.19
  180.8 0.1 collective-permute-start.1
  180.8 0.7 broadcast_select_fusion.1
  181.5 0.2 scatter-add.11
  181.7 5.8 %collective-permute-done.1.cot = bf16[64,4096]{1,0:T(8,128)(2,1)S(1)} collective-permute-done((bf16[64,4096]{1,0:T(8,128)(2,1)S(1)}, bf16[64,4096]{1,0:T(8,128)(2,1)S(1)}, u32[]{:S(2)}, u32[]{:S(2)}) %collective-permute-start.1) | collective-permute-done | bytes 524320 | tf_op jit(solution)/shard_map/ppermute | solution.py:20
  187.5 0.8 copy-done.9
  188.3 4.4 %shard_map.90 = (bf16[64,1024]{1,0:T(8,128)(2,1)}, bf16[64,4096]{1,0:T(8,128)(2,1)}) custom-call(bf16[64,4096]{1,0:T(8,128)(2,1)} %get-tuple-element.95.x, f32[1,4096]{1,0:T(1,128)} %get-tuple-element.101.gain, f32[64,1024]{1,0:T(8,128)} %get-tuple-element.98.raw, bf16[64,4096]{1,0:T(8,128)(2,1)} %copy-done.9, f32[64,64]{1,0:T(8,128)} %fusion.33.allowed, ...), custom_call_target="tpu_custom_call" | custom-call | flops 500000000 | bytes 3000000 | tf_op jit(solution)/shard_map/pallas_call | solution.py:427
  192.7 32.7 %shard_map.91 = (bf16[2,4,64,1024]{3,2,1,0:T(8,128)(2,1)}, bf16[64,4096]{1,0:T(8,128)(2,1)}) custom-call(bf16[64,1024]{1,0:T(8,128)(2,1)} %get-tuple-element.67.kc, bf16[2,1024,1024]{2,1,0:T(8,128)(2,1)} %get-tuple-element.61.w2), custom_call_target="tpu_custom_call" | custom-call | tf_op jit(solution)/shard_map/pallas_call | solution.py:293
  225.5 1.6 fusion.17
  227.1 0.7 broadcast_select_fusion
  227.8 0.2 scatter-add.14
  227.9 0.0 copy-start.13
  227.9 0.6 copy-done.13
  228.6 10.5 %shard_map.92 = (bf16[2,512,1024]{2,1,0:T(8,128)(2,1)}, f32[2,512]{1,0:T(2,128)}) custom-call(f32[8,2,512]{2,1,0:T(2,128)} %bitcast.79, bf16[2,4,3,64,512]{4,3,2,1,0:T(8,128)(2,1)} %get-tuple-element.69.cols, bf16[2,4,64,1024]{3,2,1,0:T(8,128)(2,1)} %get-tuple-element.70.first, bf16[2,4,64,1024]{3,2,1,0:T(8,128)(2,1)} %get-tuple-element.71.second, ...), custom_call_target="tpu_custom_call" | custom-call | tf_op jit(solution)/shard_map/pallas_call | solution.py:347
  239.0 1.4 convert_bitcast_fusion.2
  240.4 1.3 fusion.21
  241.8 1.3 copy.21
  (49 shorter events, 0.2 us)
Async XLA Ops:
  0.8 3.8 %copy-start.19 = (bf16[2,1,512]{2,0,1:T(2,128)(2,1)S(1)}, bf16[2,1,512]{2,0,1:T(2,128)(2,1)}, u32[]{:S(2)}) copy-start(bf16[2,1,512]{2,0,1:T(2,128)(2,1)} %param.15) | copy-start | bytes 6148
  0.8 4.4 %copy-start.18 = (s32[4,1]{0,1:T(1,128)S(1)}, s32[4,1]{0,1:T(1,128)}, u32[]{:S(2)}) copy-start(s32[4,1]{0,1:T(1,128)} %param.16) | copy-start | bytes 52
  0.8 7.0 %copy-start.20 = (s32[4,1,64]{2,1,0:T(1,128)S(1)}, s32[4,1,64]{2,1,0:T(1,128)}, u32[]{:S(2)}) copy-start(s32[4,1,64]{2,1,0:T(1,128)} %param.17) | copy-start | bytes 3076
  88.7 2.8 %copy-start.17 = (f32[8,2,512]{2,1,0:T(2,128)S(1)}, f32[8,2,512]{2,1,0:T(2,128)}, u32[]{:S(2)}) copy-start(f32[8,2,512]{2,1,0:T(2,128)} %get-tuple-element.57) | copy-start | bytes 98308
  96.5 32.3 %copy-start = (bf16[1,1,3,64,4096]{4,3,2,1,0:T(8,128)(2,1)S(1)}, bf16[1,1,3,64,4096]{4,3,2,1,0:T(8,128)(2,1)}, u32[]{:S(2)}) copy-start(bf16[1,1,3,64,4096]{4,3,2,1,0:T(8,128)(2,1)} %param.12) | copy-start | bytes 4718596
  96.5 32.3 %copy-start.5 = (bf16[64,4096]{1,0:T(8,128)(2,1)S(1)}, bf16[64,4096]{1,0:T(8,128)(2,1)}, u32[]{:S(2)}) copy-start(bf16[64,4096]{1,0:T(8,128)(2,1)} %get-tuple-element.59) | copy-start | bytes 1572868
  96.5 32.3 %copy-start.16 = (f32[1,4096]{1,0:T(1,128)S(1)}, f32[1,4096]{1,0:T(1,128)}, u32[]{:S(2)}) copy-start(f32[1,4096]{1,0:T(1,128)} %get-tuple-element.103.gain) | copy-start | bytes 49156
  128.7 1.8 copy-start.7
  128.8 1.8 copy-start.8
  130.6 4.9 %copy-start.21 = (s32[2]{0:T(128)S(1)}, s32[2]{0:T(128)}, u32[]{:S(2)}) copy-start(s32[2]{0:T(128)} %constant.155.clone.1) | copy-start | bytes 28
  131.2 8.1 %collective-permute-start = (bf16[64,4096]{1,0:T(8,128)(2,1)S(1)}, bf16[64,4096]{1,0:T(8,128)(2,1)S(1)}, u32[]{:S(2)}, u32[]{:S(2)}) collective-permute-start(bf16[64,4096]{1,0:T(8,128)(2,1)S(1)} %fusion.20), channel_id=1, source_target_pairs={{0,24},{8,0},{16,8},{24,16},{1,25},{9,1},{17,9},{25,17},{2,26},{10... | collective-permute-start | bytes 1572872 | tf_op jit(solution)/shard_map/ppermute | solution.py:20
  139.3 0.8 copy-start.11
  144.5 33.9 %copy-start.4 = (bf16[64,4096]{1,0:T(8,128)(2,1)S(1)}, bf16[64,4096]{1,0:T(8,128)(2,1)}, u32[]{:S(2)}) copy-start(bf16[64,4096]{1,0:T(8,128)(2,1)} %get-tuple-element.63) | copy-start | bytes 1572868
  144.5 33.9 %copy-start.15 = (f32[1,4096]{1,0:T(1,128)S(1)}, f32[1,4096]{1,0:T(1,128)}, u32[]{:S(2)}) copy-start(f32[1,4096]{1,0:T(1,128)} %get-tuple-element.102.gain) | copy-start | bytes 49156
  178.4 1.8 copy-start.6
  178.4 1.8 copy-start.12
  180.8 6.8 %collective-permute-start.1 = (bf16[64,4096]{1,0:T(8,128)(2,1)S(1)}, bf16[64,4096]{1,0:T(8,128)(2,1)S(1)}, u32[]{:S(2)}, u32[]{:S(2)}) collective-permute-start(bf16[64,4096]{1,0:T(8,128)(2,1)S(1)} %fusion.19), channel_id=1, source_target_pairs={{0,24},{8,0},{16,8},{24,16},{1,25},{9,1},{17,9},{25,17},{2,26},{10... | collective-permute-start | bytes 1572872 | tf_op jit(solution)/shard_map/ppermute | solution.py:20
  187.5 0.8 copy-start.9
  192.7 32.7 %copy-start.2 = (bf16[64,4096]{1,0:T(8,128)(2,1)S(1)}, bf16[64,4096]{1,0:T(8,128)(2,1)}, u32[]{:S(2)}) copy-start(bf16[64,4096]{1,0:T(8,128)(2,1)} %get-tuple-element.66) | copy-start | bytes 1572868
  192.7 32.8 %copy-start.14 = (f32[1,4096]{1,0:T(1,128)S(1)}, f32[1,4096]{1,0:T(1,128)}, u32[]{:S(2)}) copy-start(f32[1,4096]{1,0:T(1,128)} %get-tuple-element.101.gain) | copy-start | bytes 49156
  227.9 0.6 copy-start.13
  228.5 11.9 %copy-start.3 = (bf16[64,4096]{1,0:T(8,128)(2,1)S(1)}, bf16[64,4096]{1,0:T(8,128)(2,1)}, u32[]{:S(2)}) copy-start(bf16[64,4096]{1,0:T(8,128)(2,1)} %get-tuple-element.68) | copy-start | bytes 1572868
  228.5 11.9 %copy-start.10 = (bf16[64,4096]{1,0:T(8,128)(2,1)S(1)}, bf16[64,4096]{1,0:T(8,128)(2,1)}, u32[]{:S(2)}) copy-start(bf16[64,4096]{1,0:T(8,128)(2,1)} %copy-done.9) | copy-start | bytes 1572868
  239.0 2.8 %copy-start.1 = (bf16[2,512,1024]{2,1,0:T(8,128)(2,1)S(1)}, bf16[2,512,1024]{2,1,0:T(8,128)(2,1)}, u32[]{:S(2)}) copy-start(bf16[2,512,1024]{2,1,0:T(8,128)(2,1)} %get-tuple-element.73) | copy-start | bytes 6291460

commit v5 on v4

--- a/solution.py
+++ b/solution.py
@@ -224,7 +224,7 @@
 
 
 def back_kernel(
-    n, sections, tick, kc, w2, rows_all, total, part, ks, kr, fs, fr, ps, pr
+    n, sections, tick, kc, w2, rows_all, total, part, ks, kr, ls, fs, fr, ps, pr
 ):
     me = lax.axis_index("fsdp")
     section = lax.axis_index("pipe")
@@ -236,9 +236,19 @@
     mine = pl.ds(pl.multiple_of(place * wide, wide), wide)
     greet_all(n, me)
 
-    def row_copy(k):
-        to = lax.rem(place + k, steps) * 2 + half
-        return to_peer(kc, rows_all.at[0, k], ks.at[k], kr.at[k], to)
+    def right(d):
+        to = lax.rem(place + 1, steps) * 2 + half
+        return to_peer(
+            rows_all.at[0, d], rows_all.at[0, d + 1], ks.at[d], kr.at[d + 1], to
+        )
+
+    def left(d):
+        to = lax.rem(place + steps - 1, steps) * 2 + half
+        slot = steps - d - 1
+        return to_peer(
+            rows_all.at[0, lax.rem(steps - d, steps)], rows_all.at[0, slot],
+            ls.at[d], kr.at[slot], to,
+        )
 
     def own_copy():
         return to_peer(kc, rows_all.at[1, 0], fs.at[0], fr.at[0], buddy)
@@ -250,13 +260,18 @@
         to = lax.rem(place - k + steps, steps) * 2 + half
         return to_peer(part.at[k], total.at[:, mine], ps.at[k], pr.at[k], to)
 
-    def send(k, _):
-        row_copy(k).start()
-        return 0
-
-    lax.fori_loop(1, steps, send, 0)
+    rows_all[0, 0] = kc[...]
+    has_right, has_left = place + 1 < steps, place >= 1
+
+    @pl.when(has_right)
+    def _():
+        right(0).start()
+
+    @pl.when(has_left)
+    def _():
+        left(0).start()
+
     own_copy().start()
-    rows_all[0, 0] = kc[...]
 
     def share(k):
         return lax.dot_general(
@@ -266,20 +281,49 @@
 
     total[:, mine] = share(0)
 
-    def answer(k, _):
-        row_copy(k).wait_recv()
+    def handle(k):
         pair_copy(k).start()
         part[k] = share(k)
         back_copy(k).start()
+
+    def answer(d, _):
+        @pl.when(place >= d)
+        def _():
+            right(d - 1).wait_recv()
+
+            @pl.when(has_right)
+            def _():
+                right(d).start()
+
+            handle(d)
+
+        @pl.when(place + d < steps)
+        def _():
+            left(d - 1).wait_recv()
+
+            @pl.when(has_left)
+            def _():
+                left(d).start()
+
+            handle(steps - d)
+
         return 0
 
     lax.fori_loop(1, steps, answer, 0)
     own_copy().wait()
 
     def finish(k, _):
-        row_copy(k).wait_send()
         pair_copy(k).wait()
         back_copy(k).wait()
+
+        @pl.when((place >= k - 1) & has_right)
+        def _():
+            right(k - 1).wait_send()
+
+        @pl.when((place + k - 1 < steps) & has_left)
+        def _():
+            left(k - 1).wait_send()
+
         return 0
 
     lax.fori_loop(1, steps, finish, 0)
@@ -299,7 +343,7 @@
         in_specs=[vmem] * 2,
         out_specs=(vmem,) * 2,
         scratch_shapes=[pltpu.VMEM((steps, rows, wide), jnp.bfloat16)]
-        + [pltpu.SemaphoreType.DMA((steps,))] * 6,
+        + [pltpu.SemaphoreType.DMA((steps,))] * 7,
         compiler_params=pltpu.CompilerParams(
             collective_id=1 + tick, has_side_effects=True, vmem_limit_bytes=LIMIT
         ),

time: 244 us -> 249 us (1.020)
  Pallas kernels: 203 us -> 208 us
    pallas_call x3, Pallas kernels: 98.8 us -> 103 us  [back(): pl.pallas_call(functools.partial(back_kernel, n, sections, tick), out_sha...]
where the time goes in v5:
time: 249 us; the launch traced here: 248 us
  Pallas kernels  208 us (84%)
  other arithmetic  21.4 us (9%)
  local copies, waits for them, and re-layouts  11.5 us (5%)
  waiting for transfers between devices  5.83 us (2%)
    pallas_call x3, Pallas kernels, back(): pl.pallas_call(functools.partial(back_kernel, n, sections, tick), out_sha...  103 us
    pallas_call x1, Pallas kernels, front(): pl.pallas_call(functools.partial(front_kernel, n, sections), out_shape=(j...  80.9 us
    pallas_call x3, Pallas kernels, attend_back(): pl.pallas_call(attend_kernel, out_shape=(jax.ShapeDtypeStruct(raw.shape,...  13.2 us
    pallas_call x1, Pallas kernels, tail(): pl.pallas_call(functools.partial(tail_kernel, n, sections), out_shape=(ja...  10.8 us
    ppermute x2, waiting for transfers between devices, passed_along(): lax.ppermute(value, axis, [(i, (i + by) % size) for i in range(size)])  5.83 us
    reduce_sum x3, other arithmetic, normalize(): return resid * factor * gain  5.17 us
  transfers between devices with their start and end apart: 2, of which 1 were waited for; matrix products, arithmetic and copies ran while one was open for 4% of the time, Pallas kernels for 0%

profile of v5, /device:TPU:0, one launch (start us, length us, event | category | flops | bytes accessed | tf_op | source)
XLA Modules:
  0.0 248.0 jit_solution(15075280144837728726)
XLA Ops:
  0.8 2.6 %slice_bitcast_fusion = (bf16[64,4096]{1,0:T(8,128)(2,1)}, bf16[64,4096]{1,0:T(8,128)(2,1)}, bf16[64,4096]{1,0:T(8,128)(2,1)}) fusion(bf16[1,1,3,64,4096]{4,3,2,1,0:T(8,128)(2,1)} %param.12), kind=kLoop, calls=%fused_computation.40 | loop fusion | bytes 3145728 | tf_op jit(solution)/shard_map/squeeze | solution.py:517
  3.4 1.2 fusion.6
  4.6 0.6 convert_bitcast_fusion
  5.2 0.7 constant_dynamic-slice_fusion
  5.9 0.6 iota_compare_fusion.7
  6.5 1.3 fusion.35.valid
  7.8 80.9 %shard_map.85 = (f32[3,64,1024]{2,1,0:T(8,128)}, bf16[2,4,3,64,512]{4,3,2,1,0:T(8,128)(2,1)}, f32[8,2,512]{2,1,0:T(2,128)}, bf16[2,1024,1024]{2,1,0:T(8,128)(2,1)}) custom-call(bf16[3,64,4096]{2,1,0:T(8,128)(2,1)} %bitcast.75, bf16[2,512,1024]{2,1,0:T(8,128)(2,1)} %bitcast.76, f32[2,512]{1,0:T(2,128)} %get-tuple-element.105.g), custom_call_target="tpu_custom_call" | custom-call | tf_op jit(solution)/shard_map/pallas_call | solution.py:200
  88.7 2.1 slice_bitcast_fusion.3
  90.8 0.7 fusion.29.allowed
  91.5 0.7 constant_dynamic-slice_fusion.2
  92.1 4.4 %shard_map.86 = (bf16[64,1024]{1,0:T(8,128)(2,1)}, bf16[64,4096]{1,0:T(8,128)(2,1)}) custom-call(bf16[64,4096]{1,0:T(8,128)(2,1)} %get-tuple-element.96.x, f32[1,4096]{1,0:T(1,128)} %get-tuple-element.103.gain, f32[64,1024]{1,0:T(8,128)} %get-tuple-element.100.raw, bf16[64,4096]{1,0:T(8,128)(2,1)} %bitcast.78, f32[64,64]{1,0:T(8,128)} %fusion.29.allowed, ...), custom_call_target="tpu_custom_call" | custom-call | flops 500000000 | bytes 3000000 | tf_op jit(solution)/shard_map/pallas_call | solution.py:471
  96.5 31.4 %shard_map.87 = (bf16[2,4,64,1024]{3,2,1,0:T(8,128)(2,1)}, bf16[64,4096]{1,0:T(8,128)(2,1)}) custom-call(bf16[64,1024]{1,0:T(8,128)(2,1)} %get-tuple-element.60.kc, bf16[2,1024,1024]{2,1,0:T(8,128)(2,1)} %get-tuple-element.61.w2), custom_call_target="tpu_custom_call" | custom-call | tf_op jit(solution)/shard_map/pallas_call | solution.py:337
  127.9 0.0 copy-start.8
  128.0 1.8 fusion.9
  129.8 0.0 copy-start.21
  129.8 0.5 fusion.20
  130.4 0.1 collective-permute-start
  130.4 0.7 iota_compare_fusion.6
  131.1 1.3 fusion.37.valid
  132.4 1.1 copy.15.g
  133.5 1.2 fusion.39.valid
  134.7 0.8 and_reduce_fusion
  135.5 0.6 select_select_fusion
  136.2 0.3 scatter-add.10
  136.5 0.6 iota_compare_fusion.5
  137.1 0.7 fusion.31.allowed
  137.8 0.7 fusion.33.allowed
  138.5 0.8 copy-done.11
  139.3 4.4 %shard_map.88 = (bf16[64,1024]{1,0:T(8,128)(2,1)}, bf16[64,4096]{1,0:T(8,128)(2,1)}) custom-call(bf16[64,4096]{1,0:T(8,128)(2,1)} %get-tuple-element.97.x, f32[1,4096]{1,0:T(1,128)} %get-tuple-element.102.gain, f32[64,1024]{1,0:T(8,128)} %get-tuple-element.99.raw, bf16[64,4096]{1,0:T(8,128)(2,1)} %copy-done.11, f32[64,64]{1,0:T(8,128)} %fusion.31.allowed, ...), custom_call_target="tpu_custom_call" | custom-call | flops 500000000 | bytes 3000000 | tf_op jit(solution)/shard_map/pallas_call | solution.py:471
  143.7 34.4 %shard_map.89 = (bf16[2,4,64,1024]{3,2,1,0:T(8,128)(2,1)}, bf16[64,4096]{1,0:T(8,128)(2,1)}) custom-call(bf16[64,1024]{1,0:T(8,128)(2,1)} %get-tuple-element.64.kc, bf16[2,1024,1024]{2,1,0:T(8,128)(2,1)} %get-tuple-element.61.w2), custom_call_target="tpu_custom_call" | custom-call | tf_op jit(solution)/shard_map/pallas_call | solution.py:337
  178.1 0.0 copy-start.12
  178.2 1.8 fusion.13
  180.0 0.5 fusion.19
  180.5 0.1 collective-permute-start.1
  180.6 0.7 broadcast_select_fusion.1
  181.3 0.2 scatter-add.11
  181.5 5.8 %collective-permute-done.1.cot = bf16[64,4096]{1,0:T(8,128)(2,1)S(1)} collective-permute-done((bf16[64,4096]{1,0:T(8,128)(2,1)S(1)}, bf16[64,4096]{1,0:T(8,128)(2,1)S(1)}, u32[]{:S(2)}, u32[]{:S(2)}) %collective-permute-start.1) | collective-permute-done | bytes 524320 | tf_op jit(solution)/shard_map/ppermute | solution.py:20
  187.3 0.8 copy-done.9
  188.1 4.4 %shard_map.90 = (bf16[64,1024]{1,0:T(8,128)(2,1)}, bf16[64,4096]{1,0:T(8,128)(2,1)}) custom-call(bf16[64,4096]{1,0:T(8,128)(2,1)} %get-tuple-element.95.x, f32[1,4096]{1,0:T(1,128)} %get-tuple-element.101.gain, f32[64,1024]{1,0:T(8,128)} %get-tuple-element.98.raw, bf16[64,4096]{1,0:T(8,128)(2,1)} %copy-done.9, f32[64,64]{1,0:T(8,128)} %fusion.33.allowed, ...), custom_call_target="tpu_custom_call" | custom-call | flops 500000000 | bytes 3000000 | tf_op jit(solution)/shard_map/pallas_call | solution.py:471
  192.5 37.3 %shard_map.91 = (bf16[2,4,64,1024]{3,2,1,0:T(8,128)(2,1)}, bf16[64,4096]{1,0:T(8,128)(2,1)}) custom-call(bf16[64,1024]{1,0:T(8,128)(2,1)} %get-tuple-element.67.kc, bf16[2,1024,1024]{2,1,0:T(8,128)(2,1)} %get-tuple-element.61.w2), custom_call_target="tpu_custom_call" | custom-call | tf_op jit(solution)/shard_map/pallas_call | solution.py:337
  229.8 1.6 fusion.17
  231.5 0.7 broadcast_select_fusion
  232.1 0.4 scatter-add.14
  232.5 0.6 copy-done.13
  233.2 10.8 %shard_map.92 = (bf16[2,512,1024]{2,1,0:T(8,128)(2,1)}, f32[2,512]{1,0:T(2,128)}) custom-call(f32[8,2,512]{2,1,0:T(2,128)} %bitcast.79, bf16[2,4,3,64,512]{4,3,2,1,0:T(8,128)(2,1)} %get-tuple-element.69.cols, bf16[2,4,64,1024]{3,2,1,0:T(8,128)(2,1)} %get-tuple-element.70.first, bf16[2,4,64,1024]{3,2,1,0:T(8,128)(2,1)} %get-tuple-element.71.second, ...), custom_call_target="tpu_custom_call" | custom-call | tf_op jit(solution)/shard_map/pallas_call | solution.py:391
  243.9 1.4 convert_bitcast_fusion.2
  245.4 1.3 fusion.21
  246.7 1.3 copy.21
  (49 shorter events, 0.2 us)
Async XLA Ops:
  0.8 3.8 %copy-start.19 = (bf16[2,1,512]{2,0,1:T(2,128)(2,1)S(1)}, bf16[2,1,512]{2,0,1:T(2,128)(2,1)}, u32[]{:S(2)}) copy-start(bf16[2,1,512]{2,0,1:T(2,128)(2,1)} %param.15) | copy-start | bytes 6148
  0.8 4.4 %copy-start.18 = (s32[4,1]{0,1:T(1,128)S(1)}, s32[4,1]{0,1:T(1,128)}, u32[]{:S(2)}) copy-start(s32[4,1]{0,1:T(1,128)} %param.16) | copy-start | bytes 52
  0.8 7.0 %copy-start.20 = (s32[4,1,64]{2,1,0:T(1,128)S(1)}, s32[4,1,64]{2,1,0:T(1,128)}, u32[]{:S(2)}) copy-start(s32[4,1,64]{2,1,0:T(1,128)} %param.17) | copy-start | bytes 3076
  88.7 2.8 %copy-start.17 = (f32[8,2,512]{2,1,0:T(2,128)S(1)}, f32[8,2,512]{2,1,0:T(2,128)}, u32[]{:S(2)}) copy-start(f32[8,2,512]{2,1,0:T(2,128)} %get-tuple-element.57) | copy-start | bytes 98308
  96.5 31.5 %copy-start = (bf16[1,1,3,64,4096]{4,3,2,1,0:T(8,128)(2,1)S(1)}, bf16[1,1,3,64,4096]{4,3,2,1,0:T(8,128)(2,1)}, u32[]{:S(2)}) copy-start(bf16[1,1,3,64,4096]{4,3,2,1,0:T(8,128)(2,1)} %param.12) | copy-start | bytes 4718596
  96.5 31.5 %copy-start.5 = (bf16[64,4096]{1,0:T(8,128)(2,1)S(1)}, bf16[64,4096]{1,0:T(8,128)(2,1)}, u32[]{:S(2)}) copy-start(bf16[64,4096]{1,0:T(8,128)(2,1)} %get-tuple-element.59) | copy-start | bytes 1572868
  96.5 31.5 %copy-start.16 = (f32[1,4096]{1,0:T(1,128)S(1)}, f32[1,4096]{1,0:T(1,128)}, u32[]{:S(2)}) copy-start(f32[1,4096]{1,0:T(1,128)} %get-tuple-element.103.gain) | copy-start | bytes 49156
  127.9 1.8 copy-start.7
  127.9 1.8 copy-start.8
  129.8 4.9 %copy-start.21 = (s32[2]{0:T(128)S(1)}, s32[2]{0:T(128)}, u32[]{:S(2)}) copy-start(s32[2]{0:T(128)} %constant.155.clone.1) | copy-start | bytes 28
  130.4 8.1 %collective-permute-start = (bf16[64,4096]{1,0:T(8,128)(2,1)S(1)}, bf16[64,4096]{1,0:T(8,128)(2,1)S(1)}, u32[]{:S(2)}, u32[]{:S(2)}) collective-permute-start(bf16[64,4096]{1,0:T(8,128)(2,1)S(1)} %fusion.20), channel_id=1, source_target_pairs={{0,24},{8,0},{16,8},{24,16},{1,25},{9,1},{17,9},{25,17},{2,26},{10... | collective-permute-start | bytes 1572872 | tf_op jit(solution)/shard_map/ppermute | solution.py:20
  138.5 0.8 copy-start.11
  143.7 34.5 %copy-start.4 = (bf16[64,4096]{1,0:T(8,128)(2,1)S(1)}, bf16[64,4096]{1,0:T(8,128)(2,1)}, u32[]{:S(2)}) copy-start(bf16[64,4096]{1,0:T(8,128)(2,1)} %get-tuple-element.63) | copy-start | bytes 1572868
  143.7 34.5 %copy-start.15 = (f32[1,4096]{1,0:T(1,128)S(1)}, f32[1,4096]{1,0:T(1,128)}, u32[]{:S(2)}) copy-start(f32[1,4096]{1,0:T(1,128)} %get-tuple-element.102.gain) | copy-start | bytes 49156
  178.1 1.8 copy-start.6
  178.1 1.8 copy-start.12
  180.5 6.8 %collective-permute-start.1 = (bf16[64,4096]{1,0:T(8,128)(2,1)S(1)}, bf16[64,4096]{1,0:T(8,128)(2,1)S(1)}, u32[]{:S(2)}, u32[]{:S(2)}) collective-permute-start(bf16[64,4096]{1,0:T(8,128)(2,1)S(1)} %fusion.19), channel_id=1, source_target_pairs={{0,24},{8,0},{16,8},{24,16},{1,25},{9,1},{17,9},{25,17},{2,26},{10... | collective-permute-start | bytes 1572872 | tf_op jit(solution)/shard_map/ppermute | solution.py:20
  187.3 0.8 copy-start.9
  192.5 37.4 %copy-start.2 = (bf16[64,4096]{1,0:T(8,128)(2,1)S(1)}, bf16[64,4096]{1,0:T(8,128)(2,1)}, u32[]{:S(2)}) copy-start(bf16[64,4096]{1,0:T(8,128)(2,1)} %get-tuple-element.66) | copy-start | bytes 1572868
  192.5 37.4 %copy-start.14 = (f32[1,4096]{1,0:T(1,128)S(1)}, f32[1,4096]{1,0:T(1,128)}, u32[]{:S(2)}) copy-start(f32[1,4096]{1,0:T(1,128)} %get-tuple-element.101.gain) | copy-start | bytes 49156
  232.5 0.6 copy-start.13
  233.2 12.2 %copy-start.3 = (bf16[64,4096]{1,0:T(8,128)(2,1)S(1)}, bf16[64,4096]{1,0:T(8,128)(2,1)}, u32[]{:S(2)}) copy-start(bf16[64,4096]{1,0:T(8,128)(2,1)} %get-tuple-element.68) | copy-start | bytes 1572868
  233.2 12.2 %copy-start.10 = (bf16[64,4096]{1,0:T(8,128)(2,1)S(1)}, bf16[64,4096]{1,0:T(8,128)(2,1)}, u32[]{:S(2)}) copy-start(bf16[64,4096]{1,0:T(8,128)(2,1)} %copy-done.9) | copy-start | bytes 1572868
  243.9 2.8 %copy-start.1 = (bf16[2,512,1024]{2,1,0:T(8,128)(2,1)S(1)}, bf16[2,512,1024]{2,1,0:T(8,128)(2,1)}, u32[]{:S(2)}) copy-start(bf16[2,512,1024]{2,1,0:T(8,128)(2,1)} %get-tuple-element.73) | copy-start | bytes 6291460
